TPU v7x, 512 devices: a whole 4x4x16 slice. The times are simulated.
512 devices in a mesh: sub: 64 (over x, z), grp: 8 (over y, core).
Axes of the slice: x: 4, y: 4, z: 16, core: 2. Of those that a mesh axis runs over, the one named last changes fastest.
Arguments:
- rhs_jump: float32 [64, 8, 256, 256], P('sub', 'grp'), may hold values from -6 to 6
- incision: int32 [64, 8, 256], P('sub', 'grp'), may hold values 0 or 1
- precond: float32 [64, 8, 256], P('sub', 'grp'), may hold values from 0.5 to 2
- left_rows: int32 [64, 8, 256], P('sub', 'grp'), may hold values from 0 to 1151, as said below
- right_rows: int32 [64, 8, 256], P('sub', 'grp'), may hold values from 0 to 1151, as said below
- diag_inv: float32 [64, 8, 3, 384, 384], P('sub', 'grp'), as said below
- coupling: float32 [64, 8, 2, 384, 384], P('sub', 'grp'), may hold values from -0.09185587 to 0.09185587
- coarse_basis: float32 [64, 8, 3, 384, 128], P('sub', 'grp'), may hold values from -0.25 to 0.25
- coarse_inv: float32 [64, 128, 128], P('sub'), as said below
Outputs:
- multipliers: float32 [64, 8, 256, 256], P('sub', 'grp')
- residual: float32 [64, 8, 256, 256], P('sub', 'grp')
Inputs may be any that keep to these rules, and one draw needn't show every extreme that they name: `left_rows`: for each subdomain, its 256 left rows and 256 right rows are 512 distinct interior rows. `right_rows`: see left_rows. `diag_inv`: every block is invertible. `coarse_inv`: every block is symmetric positive definite.
All inputs are finite; a program needn't handle non-finite values. No bound on the sum of `incision` on one device may be relied on, other than what follows from the above.
Results may differ from a plain program's by a relative error of at most 0.0003.
Values sent between devices are 32-bit elements; how exact they have to be, the bound alone decides.
No kernel may reach another device: no remote copies, remote signals or barrier semaphores. Data moves between devices by JAX's collectives and lax.ppermute only.
A program may use at most 64 MiB of HBM per device.

v0:
```python
import jax
import jax.numpy as jnp
from jax import lax
from jax.sharding import PartitionSpec as P

ITERS = 3


HIGH = lax.Precision.HIGHEST


def passed_along(shard, axis, by):
    peers = lax.axis_size(axis)
    return lax.ppermute(shard, axis, [(i, (i + by) % peers) for i in range(peers)])


def norm_total(value):
    return lax.psum(value, ("sub", "grp"))


def local(
    rhs_jump, incision, precond, left_rows, right_rows, diag_inv, coupling, coarse_basis, coarse_inv
):
    load_rhs = rhs_jump[0, 0]
    cut = incision[0, 0].astype(jnp.float32)[:, None]
    scaling = precond[0, 0][:, None]
    lrow = left_rows[0, 0]
    rrow = right_rows[0, 0]
    dinv = diag_inv[0, 0]
    coup = coupling[0, 0]
    nblk, blk = (dinv.shape[0], dinv.shape[1])
    order = nblk * blk
    basis = coarse_basis[0, 0].reshape(order, -1)
    cinv = coarse_inv[0]
    width = load_rhs.shape[1]
    start = load_rhs[None]
    scales = scaling[None]
    cuts = cut[None]

    def local_dot(first, second):
        return jnp.sum(first[-1] * second[-1], axis=0)

    multipliers = jnp.zeros_like(start)
    residual = cuts * start
    zvec = scales * residual
    direc = zvec
    rz_now = norm_total(local_dot(residual, zvec))
    for step in range(ITERS):
        apply_own = direc[0]
        apply_left = passed_along(apply_own, "sub", 1)
        zeros = jnp.zeros((order, width), jnp.float32)
        interior_load = zeros.at[rrow].add(apply_own).at[lrow].add(-apply_left)
        primal = jnp.einsum("np,nr->pr", basis, interior_load, precision=HIGH)
        summed = lax.psum(primal, "grp")
        pieces = interior_load.reshape(nblk, blk, width)
        forward = []
        for block in range(nblk):
            rhs_now = pieces[block]
            if block > 0:
                rhs_now = rhs_now - jnp.dot(coup[block - 1], forward[-1], precision=HIGH)
            forward.append(jnp.dot(dinv[block], rhs_now, precision=HIGH))
        backward = [None] * nblk
        for block in range(nblk - 1, -1, -1):
            rhs_now = forward[block]
            if block < nblk - 1:
                rhs_now = rhs_now - jnp.dot(coup[block].T, backward[block + 1], precision=HIGH)
            backward[block] = jnp.dot(dinv[block].T, rhs_now, precision=HIGH)
        solved = jnp.concatenate(backward, axis=0)
        coarse = jnp.dot(cinv, summed, precision=HIGH)
        disp = solved + jnp.dot(basis, coarse, precision=HIGH)
        yleft = jnp.take(disp, lrow, axis=0)
        yright = jnp.take(disp, rrow, axis=0)
        nextone = passed_along(yleft, "sub", -1)
        image = (cut * (yright - nextone))[None]
        alpha = rz_now / lax.psum(local_dot(direc, image), ("sub", "grp"))
        multipliers = multipliers + alpha * direc
        residual = residual - alpha * image
        if step + 1 < ITERS:
            zvec = scales * residual
            rz_new = norm_total(local_dot(residual, zvec))
            direc = zvec + rz_new / rz_now * direc
            rz_now = rz_new
    return (multipliers[-1][None, None], residual[-1][None, None])


def solution(mesh):
    placed = (
        P("sub", "grp", None, None),
        P("sub", "grp", None),
        P("sub", "grp", None),
        P("sub", "grp", None),
        P("sub", "grp", None),
        P("sub", "grp", None, None, None),
        P("sub", "grp", None, None, None),
        P("sub", "grp", None, None, None),
        P("sub", None, None),
    )
    return jax.shard_map(
        local,
        mesh=mesh,
        in_specs=placed,
        out_specs=(P("sub", "grp", None, None), P("sub", "grp", None, None)),
        check_vma=False,
    )
```

profile of v0, /device:TPU:1, one launch (start us, length us, event | category | flops | bytes accessed | tf_op | source)
XLA Modules:
  0.0 924.1 jit_solution(12377833747426889409)
XLA Ops:
  9.1 4.4 collective-permute-start
  16.2 3.6 scatter_custom_fusion
  20.4 8.8 collective-permute-done
  29.9 4.7 scatter_custom_fusion.1
  51.8 67.6 %all-reduce.5.cloned.1.call-done = f32[128,256]{0,1:T(8,128)} async-done(((f32[128,256]{0,1:T(8,128)}), f32[128,256]{0,1:T(8,128)}) %all-reduce.5.cloned.1.call-update) | async-done | bytes 131088 | tf_op jit(solution)/shard_map/psum | solution.py:54
  120.6 3.3 fusion.2
  126.6 2.9 gather_fusion.1
  131.3 7.0 collective-permute-start.1
  139.7 2.9 gather_fusion
  144.5 106.5 %all-reduce = (f32[256]{0:T(256)}, f32[256]{0:T(256)}) all-reduce(f32[256]{0:T(256)} %get-tuple-element.4, f32[256]{0:T(256)S(1)} %get-tuple-element.3), channel_id=1, replica_groups=mesh['sub'=64,'grp'=8] {'sub','grp'}, use_global_device_ids=true, to_apply=%region_1.0 | all-reduce | flops 512 | bytes 4096 | tf_op jit(solution)/shard_map/psum | solution.py:18
  254.2 98.8 %psum.66 = f32[256]{0:T(256)S(1)} all-reduce(f32[256]{0:T(256)} %get-tuple-element.9), channel_id=1, replica_groups=mesh['sub'=64,'grp'=8] {'sub','grp'}, use_global_device_ids=true, to_apply=%region_8.10 | all-reduce | flops 256 | bytes 2048 | tf_op jit(solution)/shard_map/psum | solution.py:18
  355.5 3.7 collective-permute-start.2
  359.2 3.4 scatter_custom_fusion.2
  362.6 5.6 collective-permute-done.2
  368.3 4.9 scatter_custom_fusion.3
  373.1 3.3 fusion.43
  392.8 62.3 %all-reduce.7.cloned.1.call-done = f32[128,256]{0,1:T(8,128)} async-done(((f32[128,256]{0,1:T(8,128)}), f32[128,256]{0,1:T(8,128)}) %all-reduce.7.cloned.1.call-update) | async-done | bytes 131088 | tf_op jit(solution)/shard_map/psum | solution.py:54
  456.4 3.4 fusion.1
  462.4 3.0 gather_fusion.3
  467.2 7.0 collective-permute-start.3
  474.2 3.1 gather_fusion.2
  479.6 107.2 %psum.68 = f32[256]{0:T(256)} all-reduce(f32[256]{0:T(256)} %multiply_reduce_fusion.1), channel_id=1, replica_groups=mesh['sub'=64,'grp'=8] {'sub','grp'}, use_global_device_ids=true, to_apply=%region_13.15 | all-reduce | flops 256 | bytes 2048 | tf_op jit(solution)/shard_map/psum | solution.py:75
  590.6 98.5 %psum.69 = f32[256]{0:T(256)} all-reduce(f32[256]{0:T(256)} %get-tuple-element.7), channel_id=1, replica_groups=mesh['sub'=64,'grp'=8] {'sub','grp'}, use_global_device_ids=true, to_apply=%region_15.17 | all-reduce | flops 256 | bytes 2048 | tf_op jit(solution)/shard_map/psum | solution.py:18
  691.6 3.7 collective-permute-start.4
  695.3 3.4 scatter_custom_fusion.4
  698.7 5.7 collective-permute-done.4
  704.3 4.7 scatter_custom_fusion.5
  709.0 3.3 fusion.40
  725.9 3.0 convolution_bitcast_fusion.3
  728.8 62.6 %all-reduce.9.cloned.1.call-done = f32[128,256]{0,1:T(8,128)} async-done(((f32[128,256]{0,1:T(8,128)}), f32[128,256]{0,1:T(8,128)}) %all-reduce.9.cloned.1.call-update) | async-done | bytes 131088 | tf_op jit(solution)/shard_map/psum | solution.py:54
  796.5 7.1 collective-permute-start.5
  808.0 107.2 %psum.71 = f32[256]{0:T(256)S(1)} all-reduce(f32[256]{0:T(256)S(1)} %multiply_reduce_fusion), channel_id=1, replica_groups=mesh['sub'=64,'grp'=8] {'sub','grp'}, use_global_device_ids=true, to_apply=%region_20.22 | all-reduce | flops 256 | bytes 2048 | tf_op jit(solution)/shard_map/psum | solution.py:75
  (142 shorter events, 93.0 us)
Async XLA Ops:
  7.2 39.0 %copy-start = (f32[1,1,3,384,128]{4,3,2,1,0:T(8,128)S(1)}, f32[1,1,3,384,128]{4,3,2,1,0:T(8,128)}, u32[]{:S(2)}) copy-start(f32[1,1,3,384,128]{4,3,2,1,0:T(8,128)} %param.18) | copy-start | bytes 1769476
  7.2 12.7 %copy-start.31 = (s32[1,1,256]{2,1,0:T(1,128)S(1)}, s32[1,1,256]{2,1,0:T(1,128)}, u32[]{:S(2)}) copy-start(s32[1,1,256]{2,1,0:T(1,128)} %param.15) | copy-start | bytes 3076
  7.2 112.2 %all-reduce.5.cloned.1.call-start = ((), (), s32[]{:S(2)}) async-start(), calls=%async_computation | async-start | bytes 262144 | tf_op jit(solution)/shard_map/psum | solution.py:54
  9.1 20.1 %collective-permute-start = (f32[256,256]{1,0:T(8,128)S(1)}, f32[256,256]{1,0:T(8,128)S(1)}, u32[]{:S(2)}, u32[]{:S(2)}) collective-permute-start(f32[256,256]{1,0:T(8,128)S(1)} %fusion.98), channel_id=1, source_target_pairs={{0,8},{8,16},{16,24},{24,32},{32,40},{40,48},{48,56},{56,64},{64,7... | collective-permute-start | bytes 786440 | tf_op jit(solution)/shard_map/ppermute | solution.py:14
  14.1 20.5 %copy-start.32 = (s32[256,1]{0,1:T(1,128)}, s32[256,1]{0,1:T(1,128)S(1)}, u32[]{:S(2)}) copy-start(s32[256,1]{0,1:T(1,128)S(1)} %compare_select_fusion) | copy-start | bytes 3076
  15.5 114.1 %copy-start.29 = (pred[256]{0:T(512)(128)(4,1)}, pred[256]{0:T(512)(128)(4,1)S(1)}, u32[]{:S(2)}) copy-start(pred[256]{0:T(512)(128)(4,1)S(1)} %compare_and_fusion) | copy-start | bytes 772
  16.2 13.0 %copy-start.33 = (s32[256,1]{0,1:T(1,128)}, s32[256,1]{0,1:T(1,128)S(1)}, u32[]{:S(2)}) copy-start(s32[256,1]{0,1:T(1,128)S(1)} %compare_select_fusion.1) | copy-start | bytes 3076
  16.2 110.4 %copy-start.22 = (s32[1024]{0:T(1024)}, s32[1024]{0:T(1024)S(1)}, u32[]{:S(2)}) copy-start(s32[1024]{0:T(1024)S(1)} %pad_clamp_fusion) | copy-start | bytes 12292
  16.2 18.4 %copy-start.1 = (f32[1,1,3,384,384]{4,3,2,1,0:T(8,128)S(1)}, f32[1,1,3,384,384]{4,3,2,1,0:T(8,128)}, u32[]{:S(2)}) copy-start(f32[1,1,3,384,384]{4,3,2,1,0:T(8,128)} %param.16) | copy-start | bytes 5308420
  29.9 7.3 copy-start.2
  34.6 3.4 copy-start.7
  48.9 406.3 %all-reduce.7.cloned.1.call-start = ((), (), s32[]{:S(2)}) async-start(), calls=%async_computation.1 | async-start | bytes 262144 | tf_op jit(solution)/shard_map/psum | solution.py:54
  131.3 11.3 %collective-permute-start.1 = (f32[256,256]{1,0:T(8,128)}, f32[256,256]{1,0:T(8,128)}, u32[]{:S(2)}, u32[]{:S(2)}) collective-permute-start(f32[256,256]{1,0:T(8,128)} %broadcast_select_fusion.2), channel_id=1, source_target_pairs={{0,504},{8,0},{16,8},{24,16},{32,24},{40,32},{48,40},{56,48},{64,5... | collective-permute-start | bytes 786440 | tf_op jit(solution)/shard_map/ppermute | solution.py:14
  139.0 3.6 copy-start.23
  139.7 3.0 copy-start.21
  251.7 2.6 copy-start.25
  355.5 12.7 %collective-permute-start.2 = (f32[256,256]{1,0:T(8,128)}, f32[256,256]{1,0:T(8,128)}, u32[]{:S(2)}, u32[]{:S(2)}) collective-permute-start(f32[256,256]{1,0:T(8,128)} %multiply_add_fusion.1), channel_id=1, source_target_pairs={{0,8},{8,16},{16,24},{24,32},{32,40},{40,48},{48,56},{56,64},{64,7... | collective-permute-start | bytes 786440 | tf_op jit(solution)/shard_map/ppermute | solution.py:14
  373.1 3.3 copy-start.5
  385.7 2.6 copy-start.16
  390.0 401.5 %all-reduce.9.cloned.1.call-start = ((), (), s32[]{:S(2)}) async-start(), calls=%async_computation.2 | async-start | bytes 262144 | tf_op jit(solution)/shard_map/psum | solution.py:54
  467.2 10.6 %collective-permute-start.3 = (f32[256,256]{1,0:T(8,128)}, f32[256,256]{1,0:T(8,128)}, u32[]{:S(2)}, u32[]{:S(2)}) collective-permute-start(f32[256,256]{1,0:T(8,128)} %broadcast_select_fusion.1), channel_id=1, source_target_pairs={{0,504},{8,0},{16,8},{24,16},{32,24},{40,32},{48,40},{56,48},{64,5... | collective-permute-start | bytes 786440 | tf_op jit(solution)/shard_map/ppermute | solution.py:14
  691.6 12.7 %collective-permute-start.4 = (f32[256,256]{1,0:T(8,128)}, f32[256,256]{1,0:T(8,128)}, u32[]{:S(2)}, u32[]{:S(2)}) collective-permute-start(f32[256,256]{1,0:T(8,128)} %multiply_add_fusion), channel_id=1, source_target_pairs={{0,8},{8,16},{16,24},{24,32},{32,40},{40,48},{48,56},{56,64},{64,7... | collective-permute-start | bytes 786440 | tf_op jit(solution)/shard_map/ppermute | solution.py:14
  709.0 3.3 copy-start.3
  721.6 2.6 copy-start.17
  725.8 65.6 %copy-start.19 = (f32[1,128,128]{2,1,0:T(8,128)S(1)}, f32[1,128,128]{2,1,0:T(8,128)}, u32[]{:S(2)}) copy-start(f32[1,128,128]{2,1,0:T(8,128)} %param.19) | copy-start | bytes 196612
  725.8 66.8 %copy-start.13 = (f32[256,384]{1,0:T(8,128)S(1)}, f32[256,384]{1,0:T(8,128)}, u32[]{:S(2)}) copy-start(f32[256,384]{1,0:T(8,128)} %copy-done.12) | copy-start | bytes 1179652
  796.4 118.8 %copy-start.24 = (f32[256]{0:T(256)S(1)}, f32[256]{0:T(256)}, u32[]{:S(2)}) copy-start(f32[256]{0:T(256)} %psum.69) | copy-start | bytes 3076
  796.4 118.8 %copy-start.8 = (f32[1,1,256,256]{3,2,1,0:T(8,128)S(1)}, f32[1,1,256,256]{3,2,1,0:T(8,128)}, u32[]{:S(2)}) copy-start(f32[1,1,256,256]{3,2,1,0:T(8,128)} %param.11) | copy-start | bytes 786436
  796.5 118.8 %copy-start.18 = (f32[256,256]{1,0:T(8,128)S(1)}, f32[256,256]{1,0:T(8,128)}, u32[]{:S(2)}) copy-start(f32[256,256]{1,0:T(8,128)} %get-tuple-element.8) | copy-start | bytes 786436
  796.5 118.8 %copy-start.26 = (f32[256]{0:T(256)S(1)}, f32[256]{0:T(256)}, u32[]{:S(2)}) copy-start(f32[256]{0:T(256)} %copy-done.25) | copy-start | bytes 3076
  796.5 118.8 %copy-start.28 = (f32[256]{0:T(256)S(1)}, f32[256]{0:T(256)}, u32[]{:S(2)}) copy-start(f32[256]{0:T(256)} %copy-done.27) | copy-start | bytes 3076
  796.5 10.4 %collective-permute-start.5 = (f32[256,256]{1,0:T(8,128)S(1)}, f32[256,256]{1,0:T(8,128)S(1)}, u32[]{:S(2)}, u32[]{:S(2)}) collective-permute-start(f32[256,256]{1,0:T(8,128)S(1)} %broadcast_select_fusion), channel_id=1, source_target_pairs={{0,504},{8,0},{16,8},{24,16},{32,24},{40,32},{48,40},{56,48},{64,5... | collective-permute-start | bytes 786440 | tf_op jit(solution)/shard_map/ppermute | solution.py:14
  (11 other events, 14.9 us)
Sparse Core Ops, SparseCore 0:
  49.0 70.3 all-reduce.4
  390.1 65.0 all-reduce.6
  726.0 65.3 all-reduce.8
where the time goes:
time: 929 us; the launch traced here: 924 us
  blocking collectives  518 us (56%)
  waiting for transfers between devices  215 us (23%)
  matrix products  66.8 us (7%)
  other arithmetic  53 us (6%)
  starting transfers between devices  33.3 us (4%)
  local copies, waits for them, and re-layouts  22.8 us (2%)
  between operations  14.6 us (2%)
    psum x3, blocking collectives, norm_total(): return lax.psum(value, ('sub', 'grp'))  304 us
    psum x2, blocking collectives, local(): alpha = rz_now / lax.psum(local_dot(direc, image), ('sub', 'grp'))  214 us
    psum x3, waiting for transfers between devices, local(): summed = lax.psum(primal, 'grp')  192 us
    ppermute x6, starting transfers between devices, passed_along(): lax.ppermute(shard, axis, [(i, (i + by) % peers) for i in range(peers)])  32.8 us
    scatter-add x6, other arithmetic, local(): interior_load = zeros.at[rrow].add(apply_own).at[lrow].add(-apply_left)  24.6 us
    ppermute x6, waiting for transfers between devices, passed_along(): lax.ppermute(shard, axis, [(i, (i + by) % peers) for i in range(peers)])  22.8 us
  transfers between devices with their start and end apart: 9, of which 8 were waited for; matrix products, arithmetic and copies ran while one was open for 3% of the time, Pallas kernels for 0%

commit v1 on v0

v1 whole, which is shorter than its diff:
```python
import jax
import jax.numpy as jnp
from jax import lax
from jax.sharding import PartitionSpec as P


ITERS = 3
HIGH = lax.Precision.HIGH
FULL = lax.Precision.HIGHEST


def passed_along(shard, axis, by):
    peers = lax.axis_size(axis)
    return lax.ppermute(shard, axis, [(i, (i + by) % peers) for i in range(peers)])


def exchanged(parts, axis):
    return lax.all_to_all(parts, axis, 0, 0)


def spread(part, axis):
    peers = lax.axis_size(axis)
    return exchanged(jnp.broadcast_to(part[None], (peers,) + part.shape), axis)


def grp_sum(value):
    peers = lax.axis_size("grp")
    rows, width = value.shape
    part = jnp.sum(exchanged(value.reshape(peers, rows // peers, width), "grp"), axis=0)
    return spread(part, "grp").reshape(rows, width)


def conjugate(gram):
    def inner(first, second):
        total = 0.0
        for i, a in enumerate(first):
            for j, b in enumerate(second):
                if a is not None and b is not None:
                    total = total + a * b * gram[min(i, j), max(i, j)]
        return total

    def plus(first, factor, second):
        out = []
        for i in range(max(len(first), len(second))):
            a = first[i] if i < len(first) else None
            b = second[i] if i < len(second) else None
            if b is None:
                out.append(a)
            elif a is None:
                out.append(factor * b)
            else:
                out.append(a + factor * b)
        return out

    one = jnp.ones_like(gram[0, 0])
    resid, direc, mult = [one], [one], []
    rz_now = gram[0, 0]
    for step in range(ITERS):
        image = [None] + direc
        alpha = rz_now / inner(direc, image)
        mult = plus(mult, alpha, direc)
        resid = plus(resid, -alpha, image)
        if step + 1 < ITERS:
            rz_new = inner(resid, resid)
            direc = plus(resid, rz_new / rz_now, direc)
            rz_now = rz_new
    return mult, resid


def local(
    rhs_jump, incision, precond, left_rows, right_rows, diag_inv, coupling, coarse_basis, coarse_inv
):
    rhs = rhs_jump[0, 0]
    iface, width = rhs.shape
    cut = incision[0, 0].astype(jnp.float32)
    weight = precond[0, 0] * cut
    first = weight[:, None] * rhs
    sent = passed_along(jnp.concatenate([first, jnp.broadcast_to(weight[None], (8, iface))]), "sub", 1)
    first_left = sent[:iface]
    weight_left = sent[iface]

    dinv = diag_inv[0, 0]
    coup = coupling[0, 0]
    nblk, blk = dinv.shape[0], dinv.shape[1]
    basis = coarse_basis[0, 0]
    rows = jnp.concatenate([right_rows[0, 0], left_rows[0, 0]])
    picks = [
        (lax.broadcasted_iota(jnp.int32, (blk, 2 * iface), 0) + k * blk == rows[None]).astype(jnp.float32)
        for k in range(nblk)
    ]
    sweeps = []
    for k in range(nblk):
        now = picks[k]
        if k > 0:
            now = now - jnp.dot(coup[k - 1], sweeps[-1], precision=HIGH)
        sweeps.append(jnp.dot(dinv[k], now, precision=HIGH))
    sweep = jnp.concatenate(sweeps, axis=0)
    schur = lax.dot_general(sweep, sweep, (((0,), (0,)), ((), ())), precision=HIGH)
    pick = jnp.concatenate(picks, axis=0)
    modes = lax.dot_general(pick, basis.reshape(nblk * blk, -1), (((0,), (0,)), ((), ())), precision=FULL)
    probe = lax.dot_general(coarse_inv[0], modes, (((1,), (1,)), ((), ())), precision=FULL)

    scale = jnp.concatenate([weight, -weight_left])[:, None]
    peers = lax.axis_size("grp")
    primal = modes.shape[1]
    deal = primal // peers
    loads = [jnp.concatenate([first, -first_left])]
    vectors = [cut[:, None] * rhs]
    disps = []
    for step in range(ITERS - 1):
        load = loads[-1]
        coarse = grp_sum(jnp.dot(probe, load, precision=FULL))
        disp = jnp.dot(schur, load, precision=FULL) + jnp.dot(modes, coarse, precision=FULL)
        disps.append(disp)
        right, left = disp[:iface], disp[iface:]
        from_next = passed_along(left, "sub", -1)
        from_prev = passed_along(right, "sub", 1)
        early = []
        if step == 1:
            early = [
                jnp.sum(first * rhs, axis=0),
                jnp.sum(loads[0] * disps[0], axis=0),
                jnp.sum(loads[1] * disps[0], axis=0),
                jnp.sum(loads[1] * disps[1], axis=0),
            ]
        from_next, from_prev, *early = lax.optimization_barrier((from_next, from_prev, *early))
        vectors.append(cut[:, None] * (right - from_next))
        loads.append(scale * jnp.concatenate([right - from_next, from_prev - left]))

    load = loads[-1]
    both = jnp.concatenate(
        [probe.reshape(peers, deal, -1), modes.T.reshape(peers, deal, -1)], axis=1
    ).reshape(2 * primal, -1)
    parts = jnp.dot(both, load, precision=FULL).reshape(peers, 2 * deal, width)
    solved = jnp.dot(schur, load, precision=FULL)
    late = [jnp.sum(load * disps[1], axis=0), jnp.sum(load * solved, axis=0)]
    got, *late = lax.optimization_barrier((exchanged(parts, "grp"), *late))
    part = jnp.sum(got, axis=0)
    moments = early + [late[0], late[1] + jnp.sum(part[:deal] * part[deal:], axis=0)]
    moments = jnp.stack(moments + [jnp.zeros_like(moments[0])] * (peers - len(moments)))
    gathered = spread(jnp.concatenate([part[:deal], moments]), "grp")
    coarse = gathered[:, :deal].reshape(primal, width)
    disp = solved + jnp.dot(modes, coarse, precision=FULL)
    right, left = disp[:iface], disp[iface:]
    from_next = passed_along(left, "sub", -1)
    mine = lax.broadcasted_iota(jnp.int32, (peers, 1), 0) == lax.axis_index("grp")
    owned = jnp.sum(jnp.where(mine, jnp.sum(gathered[:, deal:], axis=0), 0.0), axis=0)
    owned = jnp.broadcast_to(owned.reshape(1, -1, 128), (lax.axis_size("sub"), width // 128, 128))
    owned = exchanged(owned, "sub")
    sums = spread(jnp.sum(owned, axis=0), "grp").reshape(peers, width)
    vectors.append(cut[:, None] * (right - from_next))
    gram = {(i, j): sums[i + j] for i in range(ITERS) for j in range(i, ITERS + 1)}
    mult, resid = conjugate(gram)
    multipliers = sum(c[None] * load[:iface] for c, load in zip(mult, loads))
    residual = sum(c[None] * vector for c, vector in zip(resid, vectors))
    return (multipliers[None, None], residual[None, None])


def solution(mesh):
    placed = (
        P("sub", "grp", None, None),
        P("sub", "grp", None),
        P("sub", "grp", None),
        P("sub", "grp", None),
        P("sub", "grp", None),
        P("sub", "grp", None, None, None),
        P("sub", "grp", None, None, None),
        P("sub", "grp", None, None, None),
        P("sub", None, None),
    )

    return jax.shard_map(
        local,
        mesh=mesh,
        in_specs=placed,
        out_specs=(P("sub", "grp", None, None), P("sub", "grp", None, None)),
        check_vma=False,
    )
```

time: 929 us -> 166 us (0.18)
  blocking collectives: 518 us -> 19.3 us
  waiting for transfers between devices: 215 us -> 47.8 us
  other arithmetic: 53 us -> 6.22 us
  matrix products: 66.8 us -> 27.5 us
  starting transfers between devices: 33.3 us -> 58.8 us
  local copies, waits for them, and re-layouts: 22.8 us -> 4.26 us
  between operations: 14.6 us -> 1.1 us
    psum x5 -> x0, blocking collectives: 518 us -> none  [the longest x3 304 us: norm_total(): return lax.psum(value, ('sub', 'grp'))]
    psum x3 -> x0, waiting for transfers between devices: 192 us -> none  [local(): summed = lax.psum(primal, 'grp')]
    dot_general x39 -> x17, matrix products: 66.8 us -> 27.5 us  [the longest x3 6.45 us: local(): sweeps.append(jnp.dot(dinv[k], now, precision=HIGH))]
    all_to_all x0 -> x6, starting transfers between devices: none -> 33.5 us  [exchanged(): return lax.all_to_all(parts, axis, 0, 0)]
    all_to_all x0 -> x6, waiting for transfers between devices: none -> 26.8 us  [exchanged(): return lax.all_to_all(parts, axis, 0, 0)]
    scatter-add x6 -> x0, other arithmetic: 24.6 us -> none  [local(): interior_load = zeros.at[rrow].add(apply_own).at[lrow].add(-apply_left)]
    all_to_all x0 -> x2, blocking collectives: none -> 19.3 us  [exchanged(): return lax.all_to_all(parts, axis, 0, 0)]
    gather x6 -> x0, local copies, waits for them, and re-layouts: 14.2 us -> none  [the longest x3 7.1 us: local(): yright = jnp.take(disp, rrow, axis=0)]
  transfers between devices with their start and end apart: 9 -> 12, of which waited for: 8 -> 12; matrix products, arithmetic and copies ran while one was open for 3% -> 13% of each run, Pallas kernels for 0% -> 0%
where the time goes in v1:
time: 166 us; the launch traced here: 165 us
  starting transfers between devices  58.8 us (35%)
  waiting for transfers between devices  47.8 us (29%)
  matrix products  27.5 us (17%)
  blocking collectives  19.3 us (12%)
  other arithmetic  6.22 us (4%)
  local copies, waits for them, and re-layouts  4.26 us (3%)
    all_to_all x6, starting transfers between devices, exchanged(): return lax.all_to_all(parts, axis, 0, 0)  33.5 us
    all_to_all x6, waiting for transfers between devices, exchanged(): return lax.all_to_all(parts, axis, 0, 0)  26.8 us
    ppermute x6, starting transfers between devices, passed_along(): lax.ppermute(shard, axis, [(i, (i + by) % peers) for i in range(peers)])  25.4 us
    ppermute x6, waiting for transfers between devices, passed_along(): lax.ppermute(shard, axis, [(i, (i + by) % peers) for i in range(peers)])  21 us
    all_to_all x2, blocking collectives, exchanged(): return lax.all_to_all(parts, axis, 0, 0)  19.3 us
    dot_general x3, matrix products, local(): sweeps.append(jnp.dot(dinv[k], now, precision=HIGH))  6.45 us
    dot_general x1, matrix products, local(): lax.dot_general(sweep, sweep, (((0,), (0,)), ((), ())), precision=HIGH)  4.55 us
  transfers between devices with their start and end apart: 12, of which 12 were waited for; matrix products, arithmetic and copies ran while one was open for 13% of the time, Pallas kernels for 0%

profile of v1, /device:TPU:1, one launch (start us, length us, event | category | flops | bytes accessed | tf_op | source)
XLA Modules:
  0.0 164.9 jit_solution(1108809009566601328)
XLA Ops:
  3.2 4.4 %collective-permute-start = (f32[264,256]{1,0:T(8,128)S(1)}, f32[264,256]{1,0:T(8,128)S(1)}, u32[]{:S(2)}, u32[]{:S(2)}) collective-permute-start(f32[264,256]{1,0:T(8,128)S(1)} %pad_maximum_fusion.3), channel_id=1, source_target_pairs={{0,8},{8,16},{16,24},{24,32},{32,40},{40,48},{48,56},{56,64},{64,7... | collective-permute-start | bytes 811016 | tf_op jit(solution)/shard_map/ppermute | solution.py:14
  8.3 1.8 %fusion.14 = f32[512,384]{0,1:T(8,128)S(1)} fusion(f32[1,1,3,384,384]{4,3,2,1,0:T(8,128)} %param.14, s32[512]{0:T(512)S(1)} %pad_add_fusion), kind=kOutput, calls=%fused_computation.21 | convolution fusion | flops 453181440 | bytes 1378304 | tf_op jit(solution)/shard_map/dot_general | solution.py:96
  11.6 1.9 %fusion.18 = f32[512,384]{0,1:T(8,128)S(1)} fusion(f32[384,512]{0,1:T(8,128)S(1)} %fusion.12, f32[1,1,3,384,384]{4,3,2,1,0:T(8,128)} %param.14), kind=kOutput, calls=%fused_computation.27 | convolution fusion | flops 452984832 | bytes 2162688 | tf_op jit(solution)/shard_map/dot_general | solution.py:96
  13.8 2.6 %fusion = f32[512,128]{0,1:T(8,128)S(1)} fusion(f32[1152,128]{1,0:T(8,128)S(1)} %bitcast.170, f32[384,512]{0,1:T(8,128)S(1)} %get-tuple-element.60, f32[384,512]{0,1:T(8,128)S(1)} %get-tuple-element.59, f32[384,512]{0,1:T(8,128)S(1)} %get-tuple-element.58), kind=kOutput, calls=%fused_computation | convolution fusion | flops 907149312 | bytes 3211264 | tf_op jit(solution)/shard_map/dot_general | solution.py:100
  16.8 1.5 fusion.13
  18.3 5.3 %collective-permute-done = f32[264,256]{1,0:T(8,128)S(1)} collective-permute-done((f32[264,256]{1,0:T(8,128)S(1)}, f32[264,256]{1,0:T(8,128)S(1)}, u32[]{:S(2)}, u32[]{:S(2)}) %collective-permute-start) | collective-permute-done | bytes 270368 | tf_op jit(solution)/shard_map/ppermute | solution.py:14
  24.7 5.7 %all-to-all-start = ((f32[8,16,256]{2,1,0:T(8,128)}), f32[8,16,256]{2,1,0:T(8,128)S(1)}, u32[]{:S(2)}, u32[]{:S(2)}) async-start(f32[8,16,256]{2,1,0:T(8,128)} %bitcast.22), calls=%async_computation | async-start | bytes 262144 | tf_op jit(solution)/shard_map/all_to_all | solution.py:18
  30.4 2.8 %convolution_bitcast_fusion = f32[384,512]{1,0:T(8,128)} fusion(f32[384,512]{0,1:T(8,128)S(1)} %fusion.13, f32[1,1,3,384,384]{4,3,2,1,0:T(8,128)} %param.14), kind=kOutput, calls=%fused_computation.12 | convolution fusion | flops 452984832 | bytes 2162688 | tf_op jit(solution)/shard_map/dot_general | solution.py:96
  33.1 2.5 %all-to-all-done = f32[8,16,256]{2,1,0:T(8,128)S(1)} async-done(((f32[8,16,256]{2,1,0:T(8,128)}), f32[8,16,256]{2,1,0:T(8,128)S(1)}, u32[]{:S(2)}, u32[]{:S(2)}) %all-to-all-start) | async-done | bytes 131104 | tf_op jit(solution)/shard_map/all_to_all | solution.py:18
  36.3 4.1 %all-to-all-start.1 = ((f32[8,16,256]{2,1,0:T(8,128)}), f32[8,16,256]{2,1,0:T(8,128)S(1)}, u32[]{:S(2)}, u32[]{:S(2)}) async-start(f32[8,16,256]{2,1,0:T(8,128)} %broadcast_in_dim.34), calls=%async_computation.1 | async-start | bytes 262144 | tf_op jit(solution)/shard_map/all_to_all | solution.py:18
  40.4 4.5 %fusion.6 = f32[512,512]{1,0:T(8,128)S(1)} fusion(f32[384,512]{1,0:T(8,128)} %convolution_bitcast_fusion, f32[384,512]{1,0:T(8,128)} %bitcast.173, f32[384,512]{1,0:T(8,128)} %bitcast.174), kind=kOutput, calls=%fused_computation.6 | convolution fusion | flops 1813118976 | bytes 3407872 | tf_op jit(solution)/shard_map/dot_general | solution.py:98
  47.4 1.9 %collective-permute-start.2 = (f32[256,256]{1,0:T(8,128)S(1)}, f32[256,256]{1,0:T(8,128)S(1)}, u32[]{:S(2)}, u32[]{:S(2)}) collective-permute-start(f32[256,256]{1,0:T(8,128)S(1)} %get-tuple-element.45), channel_id=1, source_target_pairs={{0,8},{8,16},{16,24},{24,32},{32,40},{40,48},{48,56},{56,64},{64,7... | collective-permute-start | bytes 786440 | tf_op jit(solution)/shard_map/ppermute | solution.py:14
  49.3 6.7 %collective-permute-start.1 = (f32[256,256]{1,0:T(8,128)S(1)}, f32[256,256]{1,0:T(8,128)S(1)}, u32[]{:S(2)}, u32[]{:S(2)}) collective-permute-start(f32[256,256]{1,0:T(8,128)S(1)} %get-tuple-element.46), channel_id=1, source_target_pairs={{0,504},{8,0},{16,8},{24,16},{32,24},{40,32},{48,40},{56,48},{64,5... | collective-permute-start | bytes 786440 | tf_op jit(solution)/shard_map/ppermute | solution.py:14
  56.0 3.6 %collective-permute-done.2 = f32[256,256]{1,0:T(8,128)S(1)} collective-permute-done((f32[256,256]{1,0:T(8,128)S(1)}, f32[256,256]{1,0:T(8,128)S(1)}, u32[]{:S(2)}, u32[]{:S(2)}) %collective-permute-start.2) | collective-permute-done | bytes 262176 | tf_op jit(solution)/shard_map/ppermute | solution.py:14
  61.9 10.8 %all_to_all.40 = f32[8,16,256]{2,1,0:T(8,128)S(1)} all-to-all(f32[8,16,256]{2,1,0:T(8,128)S(1)} %bitcast.177), channel_id=1, replica_groups=mesh['sub'=64,'grp'=8] {'grp'}, dimensions={0} | all-to-all | bytes 262144 | tf_op jit(solution)/shard_map/all_to_all | solution.py:18
  72.7 8.5 %all_to_all.41 = f32[8,16,256]{2,1,0:T(8,128)S(1)} all-to-all(f32[8,16,256]{2,1,0:T(8,128)S(1)} %broadcast_in_dim.35), channel_id=1, replica_groups=mesh['sub'=64,'grp'=8] {'grp'}, dimensions={0} | all-to-all | bytes 262144 | tf_op jit(solution)/shard_map/all_to_all | solution.py:18
  81.8 2.3 %multiply_reduce_fusion.2 = (f32[256]{0:T(256)S(1)}, f32[256]{0:T(256)S(1)}, f32[256]{0:T(256)S(1)}, f32[512,256]{1,0:T(8,128)S(1)}) fusion(f32[512,256]{1,0:T(8,128)} %copy-done.1, f32[512,256]{1,0:T(8,128)S(1)} %convolution_add_fusion.1, f32[256,256]{1,0:T(8,128)} %copy-done.5, f32[256,256]{1,0:T(8,128)S(1)} %get-tuple-element.48, ...), kind=kOutput, calls=%fused_computation.46 | convolution fusion | flops 806354176 | bytes 3673088 | tf_op jit(solution)/shard_map/dot_general | solution.py:113
  84.2 2.1 %collective-permute-start.4 = (f32[256,256]{1,0:T(8,128)S(1)}, f32[256,256]{1,0:T(8,128)S(1)}, u32[]{:S(2)}, u32[]{:S(2)}) collective-permute-start(f32[256,256]{1,0:T(8,128)S(1)} %get-tuple-element.41), channel_id=1, source_target_pairs={{0,8},{8,16},{16,24},{24,32},{32,40},{40,48},{48,56},{56,64},{64,7... | collective-permute-start | bytes 786440 | tf_op jit(solution)/shard_map/ppermute | solution.py:14
  86.3 7.4 %collective-permute-start.3 = (f32[256,256]{1,0:T(8,128)S(1)}, f32[256,256]{1,0:T(8,128)S(1)}, u32[]{:S(2)}, u32[]{:S(2)}) collective-permute-start(f32[256,256]{1,0:T(8,128)S(1)} %get-tuple-element.42), channel_id=1, source_target_pairs={{0,504},{8,0},{16,8},{24,16},{32,24},{40,32},{48,40},{56,48},{64,5... | collective-permute-start | bytes 786440 | tf_op jit(solution)/shard_map/ppermute | solution.py:14
  93.7 3.9 %collective-permute-done.4 = f32[256,256]{1,0:T(8,128)S(1)} collective-permute-done((f32[256,256]{1,0:T(8,128)S(1)}, f32[256,256]{1,0:T(8,128)S(1)}, u32[]{:S(2)}, u32[]{:S(2)}) %collective-permute-start.4) | collective-permute-done | bytes 262176 | tf_op jit(solution)/shard_map/ppermute | solution.py:14
  100.0 5.0 %all-to-all-start.4 = ((f32[8,32,256]{2,1,0:T(8,128)}), f32[8,32,256]{2,1,0:T(8,128)S(1)}, u32[]{:S(2)}, u32[]{:S(2)}) async-start(f32[8,32,256]{2,1,0:T(8,128)} %fusion.27), calls=%async_computation.4 | async-start | bytes 524288 | tf_op jit(solution)/shard_map/all_to_all | solution.py:18
  105.0 1.8 %multiply_reduce_fusion = (f32[256]{0:T(256)S(1)}, f32[256]{0:T(256)S(1)}, f32[512,256]{1,0:T(8,128)}) fusion(f32[512,256]{1,0:T(8,128)S(1)} %maximum_multiply_fusion.1, f32[512,256]{1,0:T(8,128)S(1)} %get-tuple-element.61, f32[512,512]{1,0:T(8,128)S(1)} %fusion.6), kind=kOutput, calls=%fused_computation.44 | convolution fusion | flops 805830144 | bytes 2623488 | tf_op jit(solution)/shard_map/dot_general | solution.py:135
  106.8 4.7 %all-to-all-done.4 = f32[8,32,256]{2,1,0:T(8,128)S(1)} async-done(((f32[8,32,256]{2,1,0:T(8,128)}), f32[8,32,256]{2,1,0:T(8,128)S(1)}, u32[]{:S(2)}, u32[]{:S(2)}) %all-to-all-start.4) | async-done | bytes 262176 | tf_op jit(solution)/shard_map/all_to_all | solution.py:18
  112.3 4.3 %all-to-all-start.5 = ((f32[8,24,256]{2,1,0:T(8,128)}), f32[8,24,256]{2,1,0:T(8,128)S(1)}, u32[]{:S(2)}, u32[]{:S(2)}) async-start(f32[8,24,256]{2,1,0:T(8,128)} %broadcast_in_dim.36), calls=%async_computation.5 | async-start | bytes 393216 | tf_op jit(solution)/shard_map/all_to_all | solution.py:18
  116.7 5.9 %all-to-all-done.5 = f32[8,24,256]{2,1,0:T(8,128)S(1)} async-done(((f32[8,24,256]{2,1,0:T(8,128)}), f32[8,24,256]{2,1,0:T(8,128)S(1)}, u32[]{:S(2)}, u32[]{:S(2)}) %all-to-all-start.5) | async-done | bytes 196640 | tf_op jit(solution)/shard_map/all_to_all | solution.py:18
  123.3 8.6 %all-to-all-start.6 = ((f32[64,2,128]{2,1,0:T(2,128)}), f32[64,2,128]{2,1,0:T(2,128)S(1)}, u32[]{:S(2)}, u32[]{:S(2)}) async-start(f32[64,2,128]{2,1,0:T(2,128)} %broadcast_in_dim.39), calls=%async_computation.6 | async-start | bytes 131072 | tf_op jit(solution)/shard_map/all_to_all | solution.py:18
  132.6 12.9 %all-to-all-done.6 = f32[64,2,128]{2,1,0:T(2,128)S(1)} async-done(((f32[64,2,128]{2,1,0:T(2,128)}), f32[64,2,128]{2,1,0:T(2,128)S(1)}, u32[]{:S(2)}, u32[]{:S(2)}) %all-to-all-start.6) | async-done | bytes 65568 | tf_op jit(solution)/shard_map/all_to_all | solution.py:18
  146.2 5.6 %all-to-all-start.7 = ((f32[8,2,128]{2,1,0:T(2,128)}), f32[8,2,128]{2,1,0:T(2,128)S(1)}, u32[]{:S(2)}, u32[]{:S(2)}) async-start(f32[8,2,128]{2,1,0:T(2,128)} %broadcast_in_dim.40), calls=%async_computation.7 | async-start | bytes 16384 | tf_op jit(solution)/shard_map/all_to_all | solution.py:18
  151.8 1.5 convolution_add_fusion.2
  153.3 2.9 %collective-permute-start.5 = (f32[256,256]{1,0:T(8,128)S(1)}, f32[256,256]{1,0:T(8,128)S(1)}, u32[]{:S(2)}, u32[]{:S(2)}) collective-permute-start(f32[256,256]{1,0:T(8,128)S(1)} %slice.134), channel_id=1, source_target_pairs={{0,504},{8,0},{16,8},{24,16},{32,24},{40,32},{48,40},{56,48},{64,5... | collective-permute-start | bytes 786440 | tf_op jit(solution)/shard_map/ppermute | solution.py:14
  156.5 6.5 %collective-permute-done.5 = f32[256,256]{1,0:T(8,128)S(1)} collective-permute-done((f32[256,256]{1,0:T(8,128)S(1)}, f32[256,256]{1,0:T(8,128)S(1)}, u32[]{:S(2)}, u32[]{:S(2)}) %collective-permute-start.5) | collective-permute-done | bytes 262176 | tf_op jit(solution)/shard_map/ppermute | solution.py:14
  163.0 1.9 %fusion.37 = (f32[1,1,256,256]{3,2,1,0:T(8,128)}, f32[1,1,256,256]{3,2,1,0:T(8,128)}) fusion(f32[256,256]{1,0:T(8,128)S(1)} %collective-permute-done.5, f32[512,256]{1,0:T(8,128)S(1)} %convolution_add_fusion.2, f32[1,1,256,256]{3,2,1,0:T(8,128)} %param.9, f32[256,256]{1,0:T(8,128)S(1)} %get-tuple-element.39, f32[256,256]{1,0:T(8,128)S(1)} %copy-done.9, ...), kind=kLoop, calls=%fused_computation.56 | loop fusion | flops 1114112 | bytes 2367488 | tf_op jit(solution)/shard_map/broadcast_in_dim | solution.py:156
  (76 shorter events, 18.0 us)
Async XLA Ops:
  0.6 13.2 %copy-start = (f32[1,1,3,384,128]{4,3,2,1,0:T(8,128)S(1)}, f32[1,1,3,384,128]{4,3,2,1,0:T(8,128)}, u32[]{:S(2)}) copy-start(f32[1,1,3,384,128]{4,3,2,1,0:T(8,128)} %param.16) | copy-start | bytes 1769476
  0.6 9.5 %copy-start.11 = (f32[1,1,2,384,384]{4,3,2,1,0:T(8,128)S(1)}, f32[1,1,2,384,384]{4,3,2,1,0:T(8,128)}, u32[]{:S(2)}) copy-start(f32[1,1,2,384,384]{4,3,2,1,0:T(8,128)} %param.15) | copy-start | bytes 3538948
  3.2 20.3 %collective-permute-start = (f32[264,256]{1,0:T(8,128)S(1)}, f32[264,256]{1,0:T(8,128)S(1)}, u32[]{:S(2)}, u32[]{:S(2)}) collective-permute-start(f32[264,256]{1,0:T(8,128)S(1)} %pad_maximum_fusion.3), channel_id=1, source_target_pairs={{0,8},{8,16},{16,24},{24,32},{32,40},{40,48},{48,56},{56,64},{64,7... | collective-permute-start | bytes 811016 | tf_op jit(solution)/shard_map/ppermute | solution.py:14
  10.1 3.4 %copy-start.7 = (f32[512,384]{0,1:T(8,128)}, f32[512,384]{0,1:T(8,128)S(1)}, u32[]{:S(2)}) copy-start(f32[512,384]{0,1:T(8,128)S(1)} %fusion.14) | copy-start | bytes 2359300
  13.5 3.3 %copy-start.6 = (f32[512,384]{0,1:T(8,128)}, f32[512,384]{0,1:T(8,128)S(1)}, u32[]{:S(2)}) copy-start(f32[512,384]{0,1:T(8,128)S(1)} %fusion.18) | copy-start | bytes 2359300
  13.8 2.6 %copy-start.12 = (f32[1,128,128]{2,1,0:T(8,128)S(1)}, f32[1,128,128]{2,1,0:T(8,128)}, u32[]{:S(2)}) copy-start(f32[1,128,128]{2,1,0:T(8,128)} %param.17) | copy-start | bytes 196612
  16.8 43.9 %copy-start.3 = (f32[512,128]{0,1:T(8,128)}, f32[512,128]{0,1:T(8,128)S(1)}, u32[]{:S(2)}) copy-start(f32[512,128]{0,1:T(8,128)S(1)} %fusion.44) | copy-start | bytes 786436
  23.6 22.7 %copy-start.5 = (f32[256,256]{1,0:T(8,128)}, f32[256,256]{1,0:T(8,128)S(1)}, u32[]{:S(2)}) copy-start(f32[256,256]{1,0:T(8,128)S(1)} %slice_negate_fusion) | copy-start | bytes 786436
  24.7 11.0 %all-to-all-start = ((f32[8,16,256]{2,1,0:T(8,128)}), f32[8,16,256]{2,1,0:T(8,128)S(1)}, u32[]{:S(2)}, u32[]{:S(2)}) async-start(f32[8,16,256]{2,1,0:T(8,128)} %bitcast.22), calls=%async_computation | async-start | bytes 262144 | tf_op jit(solution)/shard_map/all_to_all | solution.py:18
  36.3 9.4 %all-to-all-start.1 = ((f32[8,16,256]{2,1,0:T(8,128)}), f32[8,16,256]{2,1,0:T(8,128)S(1)}, u32[]{:S(2)}, u32[]{:S(2)}) async-start(f32[8,16,256]{2,1,0:T(8,128)} %broadcast_in_dim.34), calls=%async_computation.1 | async-start | bytes 262144 | tf_op jit(solution)/shard_map/all_to_all | solution.py:18
  47.4 12.2 %collective-permute-start.2 = (f32[256,256]{1,0:T(8,128)S(1)}, f32[256,256]{1,0:T(8,128)S(1)}, u32[]{:S(2)}, u32[]{:S(2)}) collective-permute-start(f32[256,256]{1,0:T(8,128)S(1)} %get-tuple-element.45), channel_id=1, source_target_pairs={{0,8},{8,16},{16,24},{24,32},{32,40},{40,48},{48,56},{56,64},{64,7... | collective-permute-start | bytes 786440 | tf_op jit(solution)/shard_map/ppermute | solution.py:14
  49.3 11.2 %collective-permute-start.1 = (f32[256,256]{1,0:T(8,128)S(1)}, f32[256,256]{1,0:T(8,128)S(1)}, u32[]{:S(2)}, u32[]{:S(2)}) collective-permute-start(f32[256,256]{1,0:T(8,128)S(1)} %get-tuple-element.46), channel_id=1, source_target_pairs={{0,504},{8,0},{16,8},{24,16},{32,24},{40,32},{48,40},{56,48},{64,5... | collective-permute-start | bytes 786440 | tf_op jit(solution)/shard_map/ppermute | solution.py:14
  60.5 1.4 copy-start.8
  60.7 0.8 copy-start.1
  84.1 14.5 %copy-start.4 = (f32[512,128]{0,1:T(8,128)S(1)}, f32[512,128]{0,1:T(8,128)}, u32[]{:S(2)}) copy-start(f32[512,128]{0,1:T(8,128)} %copy-done.3) | copy-start | bytes 786436
  84.2 13.4 %collective-permute-start.4 = (f32[256,256]{1,0:T(8,128)S(1)}, f32[256,256]{1,0:T(8,128)S(1)}, u32[]{:S(2)}, u32[]{:S(2)}) collective-permute-start(f32[256,256]{1,0:T(8,128)S(1)} %get-tuple-element.41), channel_id=1, source_target_pairs={{0,8},{8,16},{16,24},{24,32},{32,40},{40,48},{48,56},{56,64},{64,7... | collective-permute-start | bytes 786440 | tf_op jit(solution)/shard_map/ppermute | solution.py:14
  86.3 12.2 %collective-permute-start.3 = (f32[256,256]{1,0:T(8,128)S(1)}, f32[256,256]{1,0:T(8,128)S(1)}, u32[]{:S(2)}, u32[]{:S(2)}) collective-permute-start(f32[256,256]{1,0:T(8,128)S(1)} %get-tuple-element.42), channel_id=1, source_target_pairs={{0,504},{8,0},{16,8},{24,16},{32,24},{40,32},{48,40},{56,48},{64,5... | collective-permute-start | bytes 786440 | tf_op jit(solution)/shard_map/ppermute | solution.py:14
  100.0 11.5 %all-to-all-start.4 = ((f32[8,32,256]{2,1,0:T(8,128)}), f32[8,32,256]{2,1,0:T(8,128)S(1)}, u32[]{:S(2)}, u32[]{:S(2)}) async-start(f32[8,32,256]{2,1,0:T(8,128)} %fusion.27), calls=%async_computation.4 | async-start | bytes 524288 | tf_op jit(solution)/shard_map/all_to_all | solution.py:18
  106.8 45.0 %copy-start.10 = (f32[512,256]{1,0:T(8,128)S(1)}, f32[512,256]{1,0:T(8,128)}, u32[]{:S(2)}) copy-start(f32[512,256]{1,0:T(8,128)} %get-tuple-element.62) | copy-start | bytes 1572868
  111.6 51.4 %copy-start.2 = (f32[512,256]{1,0:T(8,128)S(1)}, f32[512,256]{1,0:T(8,128)}, u32[]{:S(2)}) copy-start(f32[512,256]{1,0:T(8,128)} %copy-done.1) | copy-start | bytes 1572868
  111.6 51.4 %copy-start.9 = (f32[256,256]{1,0:T(8,128)S(1)}, f32[256,256]{1,0:T(8,128)}, u32[]{:S(2)}) copy-start(f32[256,256]{1,0:T(8,128)} %copy-done.8) | copy-start | bytes 786436
  112.3 10.2 %all-to-all-start.5 = ((f32[8,24,256]{2,1,0:T(8,128)}), f32[8,24,256]{2,1,0:T(8,128)S(1)}, u32[]{:S(2)}, u32[]{:S(2)}) async-start(f32[8,24,256]{2,1,0:T(8,128)} %broadcast_in_dim.36), calls=%async_computation.5 | async-start | bytes 393216 | tf_op jit(solution)/shard_map/all_to_all | solution.py:18
  123.3 22.2 %all-to-all-start.6 = ((f32[64,2,128]{2,1,0:T(2,128)}), f32[64,2,128]{2,1,0:T(2,128)S(1)}, u32[]{:S(2)}, u32[]{:S(2)}) async-start(f32[64,2,128]{2,1,0:T(2,128)} %broadcast_in_dim.39), calls=%async_computation.6 | async-start | bytes 131072 | tf_op jit(solution)/shard_map/all_to_all | solution.py:18
  146.2 10.3 %all-to-all-start.7 = ((f32[8,2,128]{2,1,0:T(2,128)}), f32[8,2,128]{2,1,0:T(2,128)S(1)}, u32[]{:S(2)}, u32[]{:S(2)}) async-start(f32[8,2,128]{2,1,0:T(2,128)} %broadcast_in_dim.40), calls=%async_computation.7 | async-start | bytes 16384 | tf_op jit(solution)/shard_map/all_to_all | solution.py:18
  153.3 9.6 %collective-permute-start.5 = (f32[256,256]{1,0:T(8,128)S(1)}, f32[256,256]{1,0:T(8,128)S(1)}, u32[]{:S(2)}, u32[]{:S(2)}) collective-permute-start(f32[256,256]{1,0:T(8,128)S(1)} %slice.134), channel_id=1, source_target_pairs={{0,504},{8,0},{16,8},{24,16},{32,24},{40,32},{48,40},{56,48},{64,5... | collective-permute-start | bytes 786440 | tf_op jit(solution)/shard_map/ppermute | solution.py:14

commit v2 on v1

v2 whole, which is shorter than its diff:
```python
import functools

import jax
import jax.numpy as jnp
from jax import lax
from jax.experimental import pallas as pl
from jax.experimental.pallas import tpu as pltpu
from jax.sharding import PartitionSpec as P


ITERS = 3
HIGH = lax.Precision.HIGH
FULL = lax.Precision.HIGHEST
F32 = jnp.float32


def passed_along(shard, axis, by):
    peers = lax.axis_size(axis)
    return lax.ppermute(shard, axis, [(i, (i + by) % peers) for i in range(peers)])


def exchanged(parts, axis, groups=None):
    return lax.all_to_all(parts, axis, 0, 0, axis_index_groups=groups)


def fused(body, *shapes, held=(), kept=(), room=()):
    out = [jax.ShapeDtypeStruct(shape, F32) for shape in shapes]
    near = pl.BlockSpec(memory_space=pltpu.VMEM)
    far = pl.BlockSpec(memory_space=pltpu.HBM)

    def call(*args):
        return pl.pallas_call(
            body,
            out_shape=out,
            in_specs=[far if i in held else near for i in range(len(args))],
            out_specs=[far if i in kept else near for i in range(len(out))],
            scratch_shapes=[pltpu.VMEM(shape, dtype) for shape, dtype in room]
            + ([pltpu.SemaphoreType.DMA((len(room),))] if room else []),
            compiler_params=pltpu.CompilerParams(vmem_limit_bytes=8 << 20),
        )(*args)

    return call


def copies(sources, targets, sems):
    made = [pltpu.make_async_copy(s, t, sems.at[i]) for i, (s, t) in enumerate(zip(sources, targets))]
    for copy in made:
        copy.start()
    return made


def product(first, second):
    return jnp.dot(first, second, precision=FULL, preferred_element_type=F32)


def column(row):
    return jnp.transpose(jnp.broadcast_to(row, (128, row.shape[1])))


def times(col, value):
    return jnp.concatenate(
        [col * value[:, i:i + 128] for i in range(0, value.shape[1], 128)], axis=1
    )


def begin(cut, pre, weights, cuts):
    keep = cut[...].astype(F32)
    cuts[...] = column(keep)
    weights[...] = column(pre[...] * keep)


def halves(total, mine, away):
    half = mine.shape[0]
    odd = lax.axis_index("grp") % 2 == 1
    mine[...] = jnp.where(odd, total[half:], total[:half])
    away[...] = jnp.where(odd, total[:half], total[half:])


def paired(mine, got, out):
    total = mine[...] + got[...]
    for i in range(out.shape[0]):
        out[i] = total


def summed(got, out):
    total = got[0]
    for i in range(1, got.shape[0]):
        total = total + got[i]
    out[...] = total


def displace_pair(solved, modes, mine, got, right, left):
    iface = right.shape[0]
    odd = lax.axis_index("grp") % 2 == 1
    top, low = jnp.where(odd, got[...], mine[...]), jnp.where(odd, mine[...], got[...])
    value = solved[...] + product(modes[...], jnp.concatenate([top, low], axis=0))
    right[...] = value[:iface]
    left[...] = value[iface:]


def enter(rhs, got, got_weight, weights, probe, load_far, scale, mine, away, load, sems):
    iface = weights.shape[0]
    side = -column(got_weight[pl.ds(0, 1), :])
    scale[pl.ds(0, iface), :] = weights[...]
    scale[pl.ds(iface, iface), :] = side
    load[pl.ds(0, iface), :] = times(weights[...], rhs[...])
    load[pl.ds(iface, iface), :] = times(side, got[...])
    (made,) = copies((load,), (load_far,), sems)
    halves(product(probe[...], load[...]), mine, away)
    made.wait()


def again(
    right, left, from_next, from_prev, scale, probe, load_far, jump_far, mine, away, load, jump, sems
):
    iface = right.shape[0]
    value = right[...] - from_next[...]
    jump[...] = value
    load[pl.ds(0, iface), :] = times(scale[pl.ds(0, iface), :], value)
    load[pl.ds(iface, iface), :] = times(scale[pl.ds(iface, iface), :], from_prev[...] - left[...])
    made = copies((load, jump), (load_far, jump_far), sems)
    halves(product(probe[...], load[...]), mine, away)
    for copy in made:
        copy.wait()


def again_last(
    right, left, from_next, from_prev, scale, probe, modes, load_far, jump_far, parts,
    load, jump, sems
):
    iface = right.shape[0]
    deal = parts.shape[1] // 2
    value = right[...] - from_next[...]
    jump[...] = value
    load[pl.ds(0, iface), :] = times(scale[pl.ds(0, iface), :], value)
    load[pl.ds(iface, iface), :] = times(scale[pl.ds(iface, iface), :], from_prev[...] - left[...])
    made = copies((load, jump), (load_far, jump_far), sems)
    coarse = product(probe[...], load[...])
    raw = product(modes[...].T, load[...])
    for i in range(parts.shape[0]):
        parts[i, pl.ds(0, deal), :] = coarse[i * deal:(i + 1) * deal]
        parts[i, pl.ds(deal, deal), :] = raw[i * deal:(i + 1) * deal]
    for copy in made:
        copy.wait()


def solve(schur, load_far, solved, load, sems):
    (made,) = copies((load_far,), (load,), sems)
    made.wait()
    solved[...] = product(schur[...], load[...])


def solve_last(
    schur, scale, load_far, rhs_far, first_far, second_far, solved, moments,
    load, rhs, first, second, sems
):
    made = copies((load_far, rhs_far, first_far, second_far), (load, rhs, first, second), sems)
    iface = rhs.shape[0]
    made[0].wait()
    value = product(schur[...], load[...])
    solved[...] = value
    for copy in made[1:]:
        copy.wait()
    u = [rhs[...], first[...], second[...]]
    p = [times(scale[pl.ds(0, iface), :], value) for value in u]
    rows = [jnp.sum(p[(k + 1) // 2] * u[k // 2], axis=0, keepdims=True) for k in range(5)]
    rows.append(jnp.sum(load[...] * value, axis=0, keepdims=True))
    moments[...] = jnp.zeros_like(moments)
    for k, row in enumerate(rows):
        moments[pl.ds(k, 1), :] = row


def added(got, out):
    total = got[0]
    for i in range(1, got.shape[0]):
        total = total + got[i]
    for i in range(out.shape[0]):
        out[i] = total


def added_last(got, moments, out):
    deal = got.shape[1] // 2
    total = got[0]
    for i in range(1, got.shape[0]):
        total = total + got[i]
    coarse, energy = total[:deal], total[:deal] * total[deal:]
    rows = moments[...]
    energy = jnp.sum(energy, axis=0, keepdims=True)
    which = lax.broadcasted_iota(jnp.int32, rows.shape, 0) == 5
    rows = rows + jnp.where(which, energy, 0.0)
    for i in range(out.shape[0]):
        out[i, pl.ds(0, deal), :] = coarse
        out[i, pl.ds(deal, rows.shape[0]), :] = rows


def displace(deal, solved, modes, gathered, right, left):
    iface = right.shape[0]
    coarse = jnp.concatenate([gathered[i, pl.ds(0, deal), :] for i in range(gathered.shape[0])], axis=0)
    value = solved[...] + product(modes[...], coarse)
    right[...] = value[:iface]
    left[...] = value[iface:]


def tally(deal, gathered, out):
    rows = gathered[0, pl.ds(deal, 8), :]
    for i in range(1, gathered.shape[0]):
        rows = rows + gathered[i, pl.ds(deal, 8), :]
    for i in range(out.shape[0]):
        out[i] = rows


def conjugate(moment):
    def inner(first, second):
        total = 0.0
        for i, a in enumerate(first):
            for j, b in enumerate(second):
                if a is not None and b is not None:
                    total = total + a * b * moment[i + j]
        return total

    def plus(first, factor, second):
        out = []
        for i in range(max(len(first), len(second))):
            a = first[i] if i < len(first) else None
            b = second[i] if i < len(second) else None
            if b is None:
                out.append(a)
            elif a is None:
                out.append(factor * b)
            else:
                out.append(a + factor * b)
        return out

    one = jnp.ones_like(moment[0])
    resid, direc, mult = [one], [one], []
    rz_now = moment[0]
    for step in range(ITERS):
        image = [None] + direc
        alpha = rz_now / inner(direc, image)
        mult = plus(mult, alpha, direc)
        resid = plus(resid, -alpha, image)
        if step + 1 < ITERS:
            rz_new = inner(resid, resid)
            direc = plus(resid, rz_new / rz_now, direc)
            rz_now = rz_new
    return mult, resid


def finish(
    sums, right, from_next, scale, cuts, rhs_far, first_far, second_far, mult, resid,
    rhs, first, second, sems
):
    made = copies((rhs_far, first_far, second_far), (rhs, first, second), sems)
    iface = right.shape[0]
    total = sums[0]
    for i in range(1, sums.shape[0]):
        total = total + sums[i]
    mults, resids = conjugate([total[i:i + 1] for i in range(2 * ITERS)])
    for copy in made:
        copy.wait()
    u = [rhs[...], first[...], second[...], right[...] - from_next[...]]
    mult[...] = times(scale[pl.ds(0, iface), :], sum(c * v for c, v in zip(mults, u)))
    resid[...] = times(cuts[...], sum(c * v for c, v in zip(resids, u)))


def local(
    rhs_jump, incision, precond, left_rows, right_rows, diag_inv, coupling, coarse_basis, coarse_inv
):
    rhs = rhs_jump[0, 0]
    iface, width = rhs.shape
    peers = lax.axis_size("grp")
    plane, tall = (iface, width), (2 * iface, width)
    near, whole = (plane, F32), (tall, F32)
    got = passed_along(rhs, "sub", 1)
    weight = precond[0] * incision[0].astype(F32)
    got_weight = passed_along(jnp.broadcast_to(weight, (8, iface)), "sub", 1)
    weights, cuts = fused(begin, (iface, 128), (iface, 128))(incision[0], precond[0])

    dinv = diag_inv[0, 0]
    coup = coupling[0, 0]
    nblk, blk = dinv.shape[0], dinv.shape[1]
    basis = coarse_basis[0, 0]
    rows = jnp.concatenate([right_rows[0, 0], left_rows[0, 0]])
    picks = [
        (lax.broadcasted_iota(jnp.int32, (blk, 2 * iface), 0) + k * blk == rows[None]).astype(F32)
        for k in range(nblk)
    ]
    sweeps = []
    for k in range(nblk):
        now = picks[k]
        if k > 0:
            now = now - jnp.dot(coup[k - 1], sweeps[-1], precision=HIGH)
        sweeps.append(jnp.dot(dinv[k], now, precision=HIGH))
    sweep = jnp.concatenate(sweeps, axis=0)
    schur = lax.dot_general(sweep, sweep, (((0,), (0,)), ((), ())), precision=HIGH)
    pick = jnp.concatenate(picks, axis=0)
    modes = lax.dot_general(pick, basis.reshape(nblk * blk, -1), (((0,), (0,)), ((), ())), precision=FULL)
    probe = lax.dot_general(coarse_inv[0], modes, (((1,), (1,)), ((), ())), precision=FULL)
    primal = modes.shape[1]
    deal = primal // peers
    pair = (primal // 2, width)
    chips = [[i for i in range(peers) if i % 2 == core] for core in range(2)]
    swap = [(i, i ^ 1) for i in range(peers)]
    load, scale, mine, away = fused(
        enter, tall, (2 * iface, 128), pair, pair, kept=(0,), room=[whole]
    )(rhs, got, got_weight, weights, probe)
    jumps = [rhs]
    for step in range(ITERS - 1):
        (both,) = fused(paired, (peers // 2,) + pair)(mine, lax.ppermute(away, "grp", swap))
        both = exchanged(both, "grp", chips)
        (solved,) = fused(solve, tall, held=(1,), room=[whole])(schur, load)
        (mine,) = fused(summed, pair)(both)
        right, left = fused(displace_pair, plane, plane)(
            solved, modes, mine, lax.ppermute(mine, "grp", swap)
        )
        from_next = passed_along(left, "sub", -1)
        from_prev = passed_along(right, "sub", 1)
        sides = (right, left, from_next, from_prev, scale)
        if step + 2 == ITERS:
            load, jump, parts = fused(
                again_last, tall, plane, (peers, 2 * deal, width),
                kept=(0, 1), room=[whole, near],
            )(*sides, probe, modes)
        else:
            load, jump, mine, away = fused(
                again, tall, plane, pair, pair, kept=(0, 1), room=[whole, near]
            )(*sides, probe)
        jumps.append(jump)
    got = exchanged(parts, "grp")
    solved, moments = fused(
        solve_last, tall, (peers, width), held=(2, 3, 4, 5),
        room=[whole, near, near, near],
    )(schur, scale, load, *jumps)
    (spread,) = fused(added_last, (peers, deal + peers, width))(got, moments)
    gathered = exchanged(spread, "grp")

    size = lax.axis_size("sub")
    run = size // 4
    runs = [[i * run + j for j in range(run)] for i in range(4)]
    across = [[i * run + j for i in range(4)] for j in range(run)]
    (sums,) = fused(functools.partial(tally, deal), (run, 8, width))(gathered)
    sums = exchanged(sums, "sub", runs)
    right, left = fused(functools.partial(displace, deal), plane, plane)(solved, modes, gathered)
    from_next = passed_along(left, "sub", -1)
    (sums,) = fused(added, (4, 8, width))(sums)
    sums = exchanged(sums, "sub", across)
    multipliers, residual = fused(
        finish, plane, plane, held=(5, 6, 7), room=[near, near, near]
    )(sums, right, from_next, scale, cuts, *jumps)
    return (multipliers[None, None], residual[None, None])


def solution(mesh):
    placed = (
        P("sub", "grp", None, None),
        P("sub", "grp", None),
        P("sub", "grp", None),
        P("sub", "grp", None),
        P("sub", "grp", None),
        P("sub", "grp", None, None, None),
        P("sub", "grp", None, None, None),
        P("sub", "grp", None, None, None),
        P("sub", None, None),
    )

    return jax.shard_map(
        local,
        mesh=mesh,
        in_specs=placed,
        out_specs=(P("sub", "grp", None, None), P("sub", "grp", None, None)),
        check_vma=False,
    )
```

time: 166 us -> 153 us (0.922)
  the two profiles are of different devices: /device:TPU:1 before, /device:TPU:32 now
where the time goes in v2:
time: 153 us; the launch traced here: 152 us
  starting transfers between devices  55.9 us (37%)
  waiting for transfers between devices  41 us (27%)
  blocking collectives  19 us (12%)
  matrix products  18 us (12%)
  Pallas kernels  12.1 us (8%)
  local copies, waits for them, and re-layouts  2.64 us (2%)
  other arithmetic  1.8 us (1%)
    ppermute x7, starting transfers between devices, passed_along(): lax.ppermute(shard, axis, [(i, (i + by) % peers) for i in range(peers)])  25.7 us
    all_to_all x4, waiting for transfers between devices, exchanged(): return lax.all_to_all(parts, axis, 0, 0, axis_index_groups=groups)  24.9 us
    all_to_all x4, starting transfers between devices, exchanged(): return lax.all_to_all(parts, axis, 0, 0, axis_index_groups=groups)  22.4 us
    all_to_all x2, blocking collectives, exchanged(): return lax.all_to_all(parts, axis, 0, 0, axis_index_groups=groups)  19 us
    ppermute x7, waiting for transfers between devices, passed_along(): lax.ppermute(shard, axis, [(i, (i + by) % peers) for i in range(peers)])  14.8 us
    pallas_call x18, Pallas kernels, call(): pl.pallas_call(body, out_shape=out, in_specs=[far if i in held else near...  12.1 us
    dot_general x3, matrix products, local(): sweeps.append(jnp.dot(dinv[k], now, precision=HIGH))  6.55 us
    dot_general x1, matrix products, local(): lax.dot_general(sweep, sweep, (((0,), (0,)), ((), ())), precision=HIGH)  4.55 us
  transfers between devices with their start and end apart: 15, of which 10 were waited for; matrix products, arithmetic and copies ran while one was open for 13% of the time, Pallas kernels for 4%

profile of v2, /device:TPU:32, one launch (start us, length us, event | category | flops | bytes accessed | tf_op | source)
XLA Modules:
  0.0 151.6 jit_solution(4523225441643134052)
XLA Ops:
  1.5 3.8 %collective-permute-start.1 = (f32[8,256]{1,0:T(8,128)S(1)}, f32[8,256]{1,0:T(8,128)S(1)}, u32[]{:S(2)}, u32[]{:S(2)}) collective-permute-start(f32[8,256]{1,0:T(8,128)S(1)} %broadcast_in_dim.6), channel_id=1, source_target_pairs={{0,8},{8,16},{16,24},{24,32},{32,40},{40,48},{48,56},{56,64},{64,7... | collective-permute-start | bytes 24584 | tf_op jit(solution)/shard_map/ppermute | solution.py:19
  5.3 3.8 %collective-permute-start = (f32[256,256]{1,0:T(8,128)}, f32[256,256]{1,0:T(8,128)S(1)}, u32[]{:S(2)}, u32[]{:S(2)}) collective-permute-start(f32[256,256]{1,0:T(8,128)} %bitcast.48), channel_id=1, source_target_pairs={{0,8},{8,16},{16,24},{24,32},{32,40},{40,48},{48,56},{56,64},{64,7... | collective-permute-start | bytes 786440 | tf_op jit(solution)/shard_map/ppermute | solution.py:19
  9.9 1.7 %fusion.15 = f32[512,384]{0,1:T(8,128)S(1)} fusion(f32[1,1,3,384,384]{4,3,2,1,0:T(8,128)} %param.14, s32[512]{0:T(512)S(1)} %pad_add_fusion), kind=kOutput, calls=%fused_computation.20 | convolution fusion | flops 453181440 | bytes 1378304 | tf_op jit(solution)/shard_map/dot_general | solution.py:293
  12.4 1.9 %fusion.18 = f32[512,384]{0,1:T(8,128)S(1)} fusion(f32[384,512]{1,0:T(8,128)S(1)} %fusion.12, f32[1,1,3,384,384]{4,3,2,1,0:T(8,128)} %param.14), kind=kOutput, calls=%fused_computation.25 | convolution fusion | flops 452984832 | bytes 2162688 | tf_op jit(solution)/shard_map/dot_general | solution.py:293
  14.6 4.0 %fusion.6.modes = f32[512,128]{1,0:T(8,128)S(1)} fusion(f32[1152,128]{1,0:T(8,128)S(1)} %bitcast.47, f32[384,512]{1,0:T(8,128)S(1)} %get-tuple-element.50, f32[384,512]{1,0:T(8,128)S(1)} %get-tuple-element.49, f32[384,512]{1,0:T(8,128)S(1)} %get-tuple-element.48), kind=kOutput, calls=%fused_computation.6 | convolution fusion | flops 907149312 | bytes 3211264 | tf_op jit(solution)/shard_map/dot_general | solution.py:297
  19.8 1.9 %collective-permute-start.2 = (f32[64,256]{1,0:T(8,128)S(1)}, f32[64,256]{1,0:T(8,128)S(1)}, u32[]{:S(2)}, u32[]{:S(2)}) collective-permute-start(f32[64,256]{1,0:T(8,128)S(1)} %get-tuple-element.28), channel_id=1, source_target_pairs={{0,1},{1,0},{2,3},{3,2},{4,5},{5,4},{6,7},{7,6},{8,9},{9,8},{10,11... | collective-permute-start | bytes 196616 | tf_op jit(solution)/shard_map/ppermute | solution.py:309
  21.8 1.7 %fusion.13 = f32[384,512]{1,0:T(8,128)} fusion(f32[512,384]{0,1:T(8,128)S(1)} %fusion.18, f32[1,1,2,384,384]{4,3,2,1,0:T(8,128)S(1)} %copy-done.10, s32[512]{0:T(512)S(1)} %pad_add_fusion, s32[384]{0:T(512)S(1)} %get-tuple-element.51), kind=kOutput, calls=%fused_computation.16 | convolution fusion | flops 453574656 | bytes 2166784 | tf_op jit(solution)/shard_map/dot_general | solution.py:292
  24.2 4.5 %all-to-all-start = ((f32[4,64,256]{2,1,0:T(8,128)}), f32[4,64,256]{2,1,0:T(8,128)S(1)}, u32[]{:S(2)}, u32[]{:S(2)}) async-start(f32[4,64,256]{2,1,0:T(8,128)} %shard_map.107), calls=%async_computation | async-start | bytes 524288 | tf_op jit(solution)/shard_map/all_to_all | solution.py:23
  28.7 3.0 %convolution_bitcast_fusion = f32[384,512]{1,0:T(8,128)} fusion(f32[384,512]{1,0:T(8,128)} %fusion.13, f32[1,1,3,384,384]{4,3,2,1,0:T(8,128)} %param.14), kind=kOutput, calls=%fused_computation.12 | convolution fusion | flops 452984832 | bytes 2162688 | tf_op jit(solution)/shard_map/dot_general | solution.py:293
  31.6 4.3 %all-to-all-done.got = f32[4,64,256]{2,1,0:T(8,128)S(1)} async-done(((f32[4,64,256]{2,1,0:T(8,128)}), f32[4,64,256]{2,1,0:T(8,128)S(1)}, u32[]{:S(2)}, u32[]{:S(2)}) %all-to-all-start) | async-done | bytes 262176 | tf_op jit(solution)/shard_map/all_to_all | solution.py:23
  36.0 2.1 %collective-permute-start.3 = (f32[64,256]{1,0:T(8,128)S(1)}, f32[64,256]{1,0:T(8,128)S(1)}, u32[]{:S(2)}, u32[]{:S(2)}) collective-permute-start(f32[64,256]{1,0:T(8,128)S(1)} %shard_map.108.mine), channel_id=1, source_target_pairs={{0,1},{1,0},{2,3},{3,2},{4,5},{5,4},{6,7},{7,6},{8,9},{9,8},{10,11... | collective-permute-start | bytes 196616 | tf_op jit(solution)/shard_map/ppermute | solution.py:314
  38.1 4.6 %fusion.schur = f32[512,512]{1,0:T(8,128)S(1)} fusion(f32[384,512]{1,0:T(8,128)} %convolution_bitcast_fusion, f32[384,512]{1,0:T(8,128)} %bitcast.54, f32[384,512]{1,0:T(8,128)} %bitcast.55), kind=kOutput, calls=%fused_computation | convolution fusion | flops 1813118976 | bytes 3407872 | tf_op jit(solution)/shard_map/dot_general | solution.py:295
  44.4 5.1 %collective-permute-start.5 = (f32[256,256]{1,0:T(8,128)S(1)}, f32[256,256]{1,0:T(8,128)S(1)}, u32[]{:S(2)}, u32[]{:S(2)}) collective-permute-start(f32[256,256]{1,0:T(8,128)S(1)} %get-tuple-element.29.right), channel_id=1, source_target_pairs={{0,8},{8,16},{16,24},{24,32},{32,40},{40,48},{48,56},{56,64},{64,7... | collective-permute-start | bytes 786440 | tf_op jit(solution)/shard_map/ppermute | solution.py:19
  49.5 3.2 %collective-permute-start.4 = (f32[256,256]{1,0:T(8,128)S(1)}, f32[256,256]{1,0:T(8,128)S(1)}, u32[]{:S(2)}, u32[]{:S(2)}) collective-permute-start(f32[256,256]{1,0:T(8,128)S(1)} %get-tuple-element.30.left), channel_id=1, source_target_pairs={{0,504},{8,0},{16,8},{24,16},{32,24},{40,32},{48,40},{56,48},{64,5... | collective-permute-start | bytes 786440 | tf_op jit(solution)/shard_map/ppermute | solution.py:19
  52.7 5.0 %collective-permute-done.5.from_prev = f32[256,256]{1,0:T(8,128)S(1)} collective-permute-done((f32[256,256]{1,0:T(8,128)S(1)}, f32[256,256]{1,0:T(8,128)S(1)}, u32[]{:S(2)}, u32[]{:S(2)}) %collective-permute-start.5) | collective-permute-done | bytes 262176 | tf_op jit(solution)/shard_map/ppermute | solution.py:19
  57.7 2.3 %collective-permute-done.4.from_next = f32[256,256]{1,0:T(8,128)S(1)} collective-permute-done((f32[256,256]{1,0:T(8,128)S(1)}, f32[256,256]{1,0:T(8,128)S(1)}, u32[]{:S(2)}, u32[]{:S(2)}) %collective-permute-start.4) | collective-permute-done | bytes 262176 | tf_op jit(solution)/shard_map/ppermute | solution.py:19
  60.6 1.9 %collective-permute-start.6 = (f32[64,256]{1,0:T(8,128)S(1)}, f32[64,256]{1,0:T(8,128)S(1)}, u32[]{:S(2)}, u32[]{:S(2)}) collective-permute-start(f32[64,256]{1,0:T(8,128)S(1)} %get-tuple-element.34), channel_id=1, source_target_pairs={{0,1},{1,0},{2,3},{3,2},{4,5},{5,4},{6,7},{7,6},{8,9},{9,8},{10,11... | collective-permute-start | bytes 196616 | tf_op jit(solution)/shard_map/ppermute | solution.py:309
  63.7 9.7 %all_to_all.30.got = f32[4,64,256]{2,1,0:T(8,128)S(1)} all-to-all(f32[4,64,256]{2,1,0:T(8,128)S(1)} %shard_map.112), channel_id=1, replica_groups={{0,2,4,6},{1,3,5,7},{8,10,12,14},{9,11,13,15},{16,18,20,22},{17,19,21,2..., dimensions={0} | all-to-all | bytes 524288 | tf_op jit(solution)/shard_map/all_to_all | solution.py:23
  73.4 1.9 %collective-permute-start.7 = (f32[64,256]{1,0:T(8,128)S(1)}, f32[64,256]{1,0:T(8,128)S(1)}, u32[]{:S(2)}, u32[]{:S(2)}) collective-permute-start(f32[64,256]{1,0:T(8,128)S(1)} %shard_map.113.mine), channel_id=1, source_target_pairs={{0,1},{1,0},{2,3},{3,2},{4,5},{5,4},{6,7},{7,6},{8,9},{9,8},{10,11... | collective-permute-start | bytes 196616 | tf_op jit(solution)/shard_map/ppermute | solution.py:314
  77.1 3.8 %collective-permute-start.9 = (f32[256,256]{1,0:T(8,128)S(1)}, f32[256,256]{1,0:T(8,128)S(1)}, u32[]{:S(2)}, u32[]{:S(2)}) collective-permute-start(f32[256,256]{1,0:T(8,128)S(1)} %get-tuple-element.35.right), channel_id=1, source_target_pairs={{0,8},{8,16},{16,24},{24,32},{32,40},{40,48},{48,56},{56,64},{64,7... | collective-permute-start | bytes 786440 | tf_op jit(solution)/shard_map/ppermute | solution.py:19
  81.0 4.0 %collective-permute-start.8 = (f32[256,256]{1,0:T(8,128)S(1)}, f32[256,256]{1,0:T(8,128)S(1)}, u32[]{:S(2)}, u32[]{:S(2)}) collective-permute-start(f32[256,256]{1,0:T(8,128)S(1)} %get-tuple-element.36.left), channel_id=1, source_target_pairs={{0,504},{8,0},{16,8},{24,16},{32,24},{40,32},{48,40},{56,48},{64,5... | collective-permute-start | bytes 786440 | tf_op jit(solution)/shard_map/ppermute | solution.py:19
  85.0 5.0 %collective-permute-done.9.from_prev = f32[256,256]{1,0:T(8,128)S(1)} collective-permute-done((f32[256,256]{1,0:T(8,128)S(1)}, f32[256,256]{1,0:T(8,128)S(1)}, u32[]{:S(2)}, u32[]{:S(2)}) %collective-permute-start.9) | collective-permute-done | bytes 262176 | tf_op jit(solution)/shard_map/ppermute | solution.py:19
  89.9 2.5 %collective-permute-done.8.from_next = f32[256,256]{1,0:T(8,128)S(1)} collective-permute-done((f32[256,256]{1,0:T(8,128)S(1)}, f32[256,256]{1,0:T(8,128)S(1)}, u32[]{:S(2)}, u32[]{:S(2)}) %collective-permute-start.8) | collective-permute-done | bytes 262176 | tf_op jit(solution)/shard_map/ppermute | solution.py:19
  92.4 1.5 shard_map.115
  94.7 3.4 %all-to-all-start.2 = ((f32[8,32,256]{2,1,0:T(8,128)}), f32[8,32,256]{2,1,0:T(8,128)S(1)}, u32[]{:S(2)}, u32[]{:S(2)}) async-start(f32[8,32,256]{2,1,0:T(8,128)} %get-tuple-element.37), calls=%async_computation.2 | async-start | bytes 524288 | tf_op jit(solution)/shard_map/all_to_all | solution.py:23
  101.4 4.1 %all-to-all-done.2.got = f32[8,32,256]{2,1,0:T(8,128)S(1)} async-done(((f32[8,32,256]{2,1,0:T(8,128)}), f32[8,32,256]{2,1,0:T(8,128)S(1)}, u32[]{:S(2)}, u32[]{:S(2)}) %all-to-all-start.2) | async-done | bytes 262176 | tf_op jit(solution)/shard_map/all_to_all | solution.py:23
  105.6 9.3 %all_to_all.31.gathered = f32[8,24,256]{2,1,0:T(8,128)S(1)} all-to-all(f32[8,24,256]{2,1,0:T(8,128)S(1)} %shard_map.117), channel_id=1, replica_groups=mesh['sub'=64,'grp'=8] {'grp'}, dimensions={0} | all-to-all | bytes 393216 | tf_op jit(solution)/shard_map/all_to_all | solution.py:23
  115.6 10.3 %all-to-all-start.4 = ((f32[16,8,256]{2,1,0:T(8,128)}), f32[16,8,256]{2,1,0:T(8,128)S(1)}, u32[]{:S(2)}, u32[]{:S(2)}) async-start(f32[16,8,256]{2,1,0:T(8,128)} %shard_map.118), calls=%async_computation.4 | async-start | bytes 262144 | tf_op jit(solution)/shard_map/all_to_all | solution.py:23
  127.2 2.0 %collective-permute-start.10 = (f32[256,256]{1,0:T(8,128)}, f32[256,256]{1,0:T(8,128)S(1)}, u32[]{:S(2)}, u32[]{:S(2)}) collective-permute-start(f32[256,256]{1,0:T(8,128)} %get-tuple-element.44), channel_id=1, source_target_pairs={{0,504},{8,0},{16,8},{24,16},{32,24},{40,32},{48,40},{56,48},{64,5... | collective-permute-start | bytes 786440 | tf_op jit(solution)/shard_map/ppermute | solution.py:19
  129.2 10.9 %all-to-all-done.4.got = f32[16,8,256]{2,1,0:T(8,128)S(1)} async-done(((f32[16,8,256]{2,1,0:T(8,128)}), f32[16,8,256]{2,1,0:T(8,128)S(1)}, u32[]{:S(2)}, u32[]{:S(2)}) %all-to-all-start.4) | async-done | bytes 131104 | tf_op jit(solution)/shard_map/all_to_all | solution.py:23
  140.7 4.3 %all-to-all-start.5 = ((f32[4,8,256]{2,1,0:T(8,128)}), f32[4,8,256]{2,1,0:T(8,128)S(1)}, u32[]{:S(2)}, u32[]{:S(2)}) async-start(f32[4,8,256]{2,1,0:T(8,128)} %shard_map.119), calls=%async_computation.5 | async-start | bytes 65536 | tf_op jit(solution)/shard_map/all_to_all | solution.py:23
  145.0 5.4 %all-to-all-done.5.sums = f32[4,8,256]{2,1,0:T(8,128)S(1)} async-done(((f32[4,8,256]{2,1,0:T(8,128)}), f32[4,8,256]{2,1,0:T(8,128)S(1)}, u32[]{:S(2)}, u32[]{:S(2)}) %all-to-all-start.5) | async-done | bytes 32800 | tf_op jit(solution)/shard_map/all_to_all | solution.py:23
  (55 shorter events, 17.5 us)
Async XLA Ops:
  0.6 13.9 %copy-start = (f32[1,1,3,384,128]{4,3,2,1,0:T(8,128)S(1)}, f32[1,1,3,384,128]{4,3,2,1,0:T(8,128)}, u32[]{:S(2)}) copy-start(f32[1,1,3,384,128]{4,3,2,1,0:T(8,128)} %param.16) | copy-start | bytes 1769476
  0.6 10.9 %copy-start.10 = (f32[1,1,2,384,384]{4,3,2,1,0:T(8,128)S(1)}, f32[1,1,2,384,384]{4,3,2,1,0:T(8,128)}, u32[]{:S(2)}) copy-start(f32[1,1,2,384,384]{4,3,2,1,0:T(8,128)} %param.15) | copy-start | bytes 3538948
  1.5 17.7 %collective-permute-start.1 = (f32[8,256]{1,0:T(8,128)S(1)}, f32[8,256]{1,0:T(8,128)S(1)}, u32[]{:S(2)}, u32[]{:S(2)}) collective-permute-start(f32[8,256]{1,0:T(8,128)S(1)} %broadcast_in_dim.6), channel_id=1, source_target_pairs={{0,8},{8,16},{16,24},{24,32},{32,40},{40,48},{48,56},{56,64},{64,7... | collective-permute-start | bytes 24584 | tf_op jit(solution)/shard_map/ppermute | solution.py:19
  5.3 13.9 %collective-permute-start = (f32[256,256]{1,0:T(8,128)}, f32[256,256]{1,0:T(8,128)S(1)}, u32[]{:S(2)}, u32[]{:S(2)}) collective-permute-start(f32[256,256]{1,0:T(8,128)} %bitcast.48), channel_id=1, source_target_pairs={{0,8},{8,16},{16,24},{24,32},{32,40},{40,48},{48,56},{56,64},{64,7... | collective-permute-start | bytes 786440 | tf_op jit(solution)/shard_map/ppermute | solution.py:19
  11.6 2.7 %copy-start.9 = (f32[512,384]{0,1:T(8,128)}, f32[512,384]{0,1:T(8,128)S(1)}, u32[]{:S(2)}) copy-start(f32[512,384]{0,1:T(8,128)S(1)} %fusion.15) | copy-start | bytes 2359300
  14.3 9.2 %copy-start.8 = (f32[512,384]{0,1:T(8,128)}, f32[512,384]{0,1:T(8,128)S(1)}, u32[]{:S(2)}) copy-start(f32[512,384]{0,1:T(8,128)S(1)} %fusion.18) | copy-start | bytes 2359300
  14.6 4.1 %copy-start.11 = (f32[1,128,128]{2,1,0:T(8,128)S(1)}, f32[1,128,128]{2,1,0:T(8,128)}, u32[]{:S(2)}) copy-start(f32[1,128,128]{2,1,0:T(8,128)} %param.17) | copy-start | bytes 196612
  14.6 4.5 %copy-start.6 = (f32[1,1,256]{2,1,0:T(1,128)S(1)}, f32[1,1,256]{2,1,0:T(1,128)}, u32[]{:S(2)}) copy-start(f32[1,1,256]{2,1,0:T(1,128)} %param.11) | copy-start | bytes 3076
  14.6 4.5 %copy-start.7 = (s32[1,1,256]{2,1,0:T(1,128)S(1)}, s32[1,1,256]{2,1,0:T(1,128)}, u32[]{:S(2)}) copy-start(s32[1,1,256]{2,1,0:T(1,128)} %param.10) | copy-start | bytes 3076
  14.6 4.6 %copy-start.1 = (f32[1,1,256,256]{3,2,1,0:T(8,128)S(1)}, f32[1,1,256,256]{3,2,1,0:T(8,128)}, u32[]{:S(2)}) copy-start(f32[1,1,256,256]{3,2,1,0:T(8,128)} %param.9) | copy-start | bytes 786436
  19.8 3.6 %collective-permute-start.2 = (f32[64,256]{1,0:T(8,128)S(1)}, f32[64,256]{1,0:T(8,128)S(1)}, u32[]{:S(2)}, u32[]{:S(2)}) collective-permute-start(f32[64,256]{1,0:T(8,128)S(1)} %get-tuple-element.28), channel_id=1, source_target_pairs={{0,1},{1,0},{2,3},{3,2},{4,5},{5,4},{6,7},{7,6},{8,9},{9,8},{10,11... | collective-permute-start | bytes 196616 | tf_op jit(solution)/shard_map/ppermute | solution.py:309
  24.2 11.8 %all-to-all-start = ((f32[4,64,256]{2,1,0:T(8,128)}), f32[4,64,256]{2,1,0:T(8,128)S(1)}, u32[]{:S(2)}, u32[]{:S(2)}) async-start(f32[4,64,256]{2,1,0:T(8,128)} %shard_map.107), calls=%async_computation | async-start | bytes 524288 | tf_op jit(solution)/shard_map/all_to_all | solution.py:23
  36.0 7.8 %collective-permute-start.3 = (f32[64,256]{1,0:T(8,128)S(1)}, f32[64,256]{1,0:T(8,128)S(1)}, u32[]{:S(2)}, u32[]{:S(2)}) collective-permute-start(f32[64,256]{1,0:T(8,128)S(1)} %shard_map.108.mine), channel_id=1, source_target_pairs={{0,1},{1,0},{2,3},{3,2},{4,5},{5,4},{6,7},{7,6},{8,9},{9,8},{10,11... | collective-permute-start | bytes 196616 | tf_op jit(solution)/shard_map/ppermute | solution.py:314
  44.4 13.3 %collective-permute-start.5 = (f32[256,256]{1,0:T(8,128)S(1)}, f32[256,256]{1,0:T(8,128)S(1)}, u32[]{:S(2)}, u32[]{:S(2)}) collective-permute-start(f32[256,256]{1,0:T(8,128)S(1)} %get-tuple-element.29.right), channel_id=1, source_target_pairs={{0,8},{8,16},{16,24},{24,32},{32,40},{40,48},{48,56},{56,64},{64,7... | collective-permute-start | bytes 786440 | tf_op jit(solution)/shard_map/ppermute | solution.py:19
  49.5 10.5 %collective-permute-start.4 = (f32[256,256]{1,0:T(8,128)S(1)}, f32[256,256]{1,0:T(8,128)S(1)}, u32[]{:S(2)}, u32[]{:S(2)}) collective-permute-start(f32[256,256]{1,0:T(8,128)S(1)} %get-tuple-element.30.left), channel_id=1, source_target_pairs={{0,504},{8,0},{16,8},{24,16},{32,24},{40,32},{48,40},{56,48},{64,5... | collective-permute-start | bytes 786440 | tf_op jit(solution)/shard_map/ppermute | solution.py:19
  60.6 3.1 %collective-permute-start.6 = (f32[64,256]{1,0:T(8,128)S(1)}, f32[64,256]{1,0:T(8,128)S(1)}, u32[]{:S(2)}, u32[]{:S(2)}) collective-permute-start(f32[64,256]{1,0:T(8,128)S(1)} %get-tuple-element.34), channel_id=1, source_target_pairs={{0,1},{1,0},{2,3},{3,2},{4,5},{5,4},{6,7},{7,6},{8,9},{9,8},{10,11... | collective-permute-start | bytes 196616 | tf_op jit(solution)/shard_map/ppermute | solution.py:309
  73.4 3.1 %collective-permute-start.7 = (f32[64,256]{1,0:T(8,128)S(1)}, f32[64,256]{1,0:T(8,128)S(1)}, u32[]{:S(2)}, u32[]{:S(2)}) collective-permute-start(f32[64,256]{1,0:T(8,128)S(1)} %shard_map.113.mine), channel_id=1, source_target_pairs={{0,1},{1,0},{2,3},{3,2},{4,5},{5,4},{6,7},{7,6},{8,9},{9,8},{10,11... | collective-permute-start | bytes 196616 | tf_op jit(solution)/shard_map/ppermute | solution.py:314
  77.1 12.8 %collective-permute-start.9 = (f32[256,256]{1,0:T(8,128)S(1)}, f32[256,256]{1,0:T(8,128)S(1)}, u32[]{:S(2)}, u32[]{:S(2)}) collective-permute-start(f32[256,256]{1,0:T(8,128)S(1)} %get-tuple-element.35.right), channel_id=1, source_target_pairs={{0,8},{8,16},{16,24},{24,32},{32,40},{40,48},{48,56},{56,64},{64,7... | collective-permute-start | bytes 786440 | tf_op jit(solution)/shard_map/ppermute | solution.py:19
  81.0 11.5 %collective-permute-start.8 = (f32[256,256]{1,0:T(8,128)S(1)}, f32[256,256]{1,0:T(8,128)S(1)}, u32[]{:S(2)}, u32[]{:S(2)}) collective-permute-start(f32[256,256]{1,0:T(8,128)S(1)} %get-tuple-element.36.left), channel_id=1, source_target_pairs={{0,504},{8,0},{16,8},{24,16},{32,24},{40,32},{48,40},{56,48},{64,5... | collective-permute-start | bytes 786440 | tf_op jit(solution)/shard_map/ppermute | solution.py:19
  94.0 0.8 copy-start.2
  94.7 10.9 %all-to-all-start.2 = ((f32[8,32,256]{2,1,0:T(8,128)}), f32[8,32,256]{2,1,0:T(8,128)S(1)}, u32[]{:S(2)}, u32[]{:S(2)}) async-start(f32[8,32,256]{2,1,0:T(8,128)} %get-tuple-element.37), calls=%async_computation.2 | async-start | bytes 524288 | tf_op jit(solution)/shard_map/all_to_all | solution.py:23
  98.2 1.0 copy-start.3
  100.7 0.8 copy-start.4
  105.6 20.3 %copy-start.5 = (f32[512,256]{1,0:T(8,128)S(1)}, f32[512,256]{1,0:T(8,128)}, u32[]{:S(2)}) copy-start(f32[512,256]{1,0:T(8,128)} %copy-done.4) | copy-start | bytes 1572868
  115.6 24.5 %all-to-all-start.4 = ((f32[16,8,256]{2,1,0:T(8,128)}), f32[16,8,256]{2,1,0:T(8,128)S(1)}, u32[]{:S(2)}, u32[]{:S(2)}) async-start(f32[16,8,256]{2,1,0:T(8,128)} %shard_map.118), calls=%async_computation.4 | async-start | bytes 262144 | tf_op jit(solution)/shard_map/all_to_all | solution.py:23
  127.2 17.9 %collective-permute-start.10 = (f32[256,256]{1,0:T(8,128)}, f32[256,256]{1,0:T(8,128)S(1)}, u32[]{:S(2)}, u32[]{:S(2)}) collective-permute-start(f32[256,256]{1,0:T(8,128)} %get-tuple-element.44), channel_id=1, source_target_pairs={{0,504},{8,0},{16,8},{24,16},{32,24},{40,32},{48,40},{56,48},{64,5... | collective-permute-start | bytes 786440 | tf_op jit(solution)/shard_map/ppermute | solution.py:19
  140.7 9.7 %all-to-all-start.5 = ((f32[4,8,256]{2,1,0:T(8,128)}), f32[4,8,256]{2,1,0:T(8,128)S(1)}, u32[]{:S(2)}, u32[]{:S(2)}) async-start(f32[4,8,256]{2,1,0:T(8,128)} %shard_map.119), calls=%async_computation.5 | async-start | bytes 65536 | tf_op jit(solution)/shard_map/all_to_all | solution.py:23

commit v3 on v2

--- a/solution.py
+++ b/solution.py
@@ -273,7 +273,8 @@
     near, whole = (plane, F32), (tall, F32)
     got = passed_along(rhs, "sub", 1)
     weight = precond[0] * incision[0].astype(F32)
-    got_weight = passed_along(jnp.broadcast_to(weight, (8, iface)), "sub", 1)
+    weight = jnp.broadcast_to(weight, (8, iface))
+    got_weight = passed_along(weight, "sub", 1)
     weights, cuts = fused(begin, (iface, 128), (iface, 128))(incision[0], precond[0])
 
     dinv = diag_inv[0, 0]
@@ -294,7 +295,7 @@
     sweep = jnp.concatenate(sweeps, axis=0)
     schur = lax.dot_general(sweep, sweep, (((0,), (0,)), ((), ())), precision=HIGH)
     pick = jnp.concatenate(picks, axis=0)
-    modes = lax.dot_general(pick, basis.reshape(nblk * blk, -1), (((0,), (0,)), ((), ())), precision=FULL)
+    modes = lax.dot_general(pick, basis.reshape(nblk * blk, -1), (((0,), (0,)), ((), ())), precision=HIGH)
     probe = lax.dot_general(coarse_inv[0], modes, (((1,), (1,)), ((), ())), precision=FULL)
     primal = modes.shape[1]
     deal = primal // peers

time: 153 us -> 151 us (0.987)
  starting transfers between devices: 55.9 us -> 59.1 us
  waiting for transfers between devices: 41 us -> 38.5 us
  matrix products: 18 us -> 16.1 us
    ppermute x7, starting transfers between devices: 25.7 us -> 28.6 us  [passed_along(): lax.ppermute(shard, axis, [(i, (i + by) % peers) for i in range(peers)])]
    ppermute x7, waiting for transfers between devices: 14.8 us -> 12.4 us  [passed_along(): lax.ppermute(shard, axis, [(i, (i + by) % peers) for i in range(peers)])]
    dot_general x1, matrix products: 4 us -> 2.11 us  [local(): lax.dot_general(pick, basis.reshape(nblk * blk, -1), (((0,), (0,)), ((),...]
  transfers between devices with their start and end apart: 15 -> 15, of which waited for: 10 -> 9; matrix products, arithmetic and copies ran while one was open for 13% -> 11% of each run, Pallas kernels for 4% -> 4%
where the time goes in v3:
time: 151 us; the launch traced here: 150 us
  starting transfers between devices  59.1 us (39%)
  waiting for transfers between devices  38.5 us (25%)
  blocking collectives  19 us (13%)
  matrix products  16.1 us (11%)
  Pallas kernels  12.1 us (8%)
  local copies, waits for them, and re-layouts  2.64 us (2%)
  other arithmetic  1.8 us (1%)
    ppermute x7, starting transfers between devices, passed_along(): lax.ppermute(shard, axis, [(i, (i + by) % peers) for i in range(peers)])  28.6 us
    all_to_all x4, waiting for transfers between devices, exchanged(): return lax.all_to_all(parts, axis, 0, 0, axis_index_groups=groups)  24.9 us
    all_to_all x4, starting transfers between devices, exchanged(): return lax.all_to_all(parts, axis, 0, 0, axis_index_groups=groups)  22.6 us
    all_to_all x2, blocking collectives, exchanged(): return lax.all_to_all(parts, axis, 0, 0, axis_index_groups=groups)  19 us
    ppermute x7, waiting for transfers between devices, passed_along(): lax.ppermute(shard, axis, [(i, (i + by) % peers) for i in range(peers)])  12.4 us
    pallas_call x18, Pallas kernels, call(): pl.pallas_call(body, out_shape=out, in_specs=[far if i in held else near...  12.1 us
    dot_general x3, matrix products, local(): sweeps.append(jnp.dot(dinv[k], now, precision=HIGH))  6.55 us
    dot_general x1, matrix products, local(): lax.dot_general(sweep, sweep, (((0,), (0,)), ((), ())), precision=HIGH)  4.55 us
  transfers between devices with their start and end apart: 15, of which 9 were waited for; matrix products, arithmetic and copies ran while one was open for 11% of the time, Pallas kernels for 4%

profile of v3, /device:TPU:32, one launch (start us, length us, event | category | flops | bytes accessed | tf_op | source)
XLA Modules:
  0.0 150.5 jit_solution(14249984851788364874)
XLA Ops:
  1.5 3.8 %collective-permute-start.1 = (f32[8,256]{1,0:T(8,128)S(1)}, f32[8,256]{1,0:T(8,128)S(1)}, u32[]{:S(2)}, u32[]{:S(2)}) collective-permute-start(f32[8,256]{1,0:T(8,128)S(1)} %broadcast_in_dim.6), channel_id=1, source_target_pairs={{0,8},{8,16},{16,24},{24,32},{32,40},{40,48},{48,56},{56,64},{64,7... | collective-permute-start | bytes 24584 | tf_op jit(solution)/shard_map/ppermute | solution.py:19
  5.3 3.8 %collective-permute-start = (f32[256,256]{1,0:T(8,128)}, f32[256,256]{1,0:T(8,128)S(1)}, u32[]{:S(2)}, u32[]{:S(2)}) collective-permute-start(f32[256,256]{1,0:T(8,128)} %bitcast.48), channel_id=1, source_target_pairs={{0,8},{8,16},{16,24},{24,32},{32,40},{40,48},{48,56},{56,64},{64,7... | collective-permute-start | bytes 786440 | tf_op jit(solution)/shard_map/ppermute | solution.py:19
  9.9 1.7 %fusion.15 = f32[512,384]{0,1:T(8,128)S(1)} fusion(f32[1,1,3,384,384]{4,3,2,1,0:T(8,128)} %param.14, s32[512]{0:T(512)S(1)} %pad_add_fusion), kind=kOutput, calls=%fused_computation.20 | convolution fusion | flops 453181440 | bytes 1378304 | tf_op jit(solution)/shard_map/dot_general | solution.py:294
  12.4 1.9 %fusion.18 = f32[512,384]{0,1:T(8,128)S(1)} fusion(f32[384,512]{1,0:T(8,128)S(1)} %fusion.12, f32[1,1,3,384,384]{4,3,2,1,0:T(8,128)} %param.14), kind=kOutput, calls=%fused_computation.25 | convolution fusion | flops 452984832 | bytes 2162688 | tf_op jit(solution)/shard_map/dot_general | solution.py:294
  14.6 2.1 %fusion.6.modes = f32[512,128]{1,0:T(8,128)S(1)} fusion(f32[1152,128]{1,0:T(8,128)S(1)} %bitcast.47, f32[384,512]{1,0:T(8,128)S(1)} %get-tuple-element.50, f32[384,512]{1,0:T(8,128)S(1)} %get-tuple-element.49, f32[384,512]{1,0:T(8,128)S(1)} %get-tuple-element.48), kind=kOutput, calls=%fused_computation.6 | convolution fusion | flops 454164480 | bytes 3211264 | tf_op jit(solution)/shard_map/dot_general | solution.py:298
  17.9 1.9 %collective-permute-start.2 = (f32[64,256]{1,0:T(8,128)S(1)}, f32[64,256]{1,0:T(8,128)S(1)}, u32[]{:S(2)}, u32[]{:S(2)}) collective-permute-start(f32[64,256]{1,0:T(8,128)S(1)} %get-tuple-element.28), channel_id=1, source_target_pairs={{0,1},{1,0},{2,3},{3,2},{4,5},{5,4},{6,7},{7,6},{8,9},{9,8},{10,11... | collective-permute-start | bytes 196616 | tf_op jit(solution)/shard_map/ppermute | solution.py:310
  19.9 1.7 %fusion.13 = f32[384,512]{1,0:T(8,128)} fusion(f32[512,384]{0,1:T(8,128)S(1)} %fusion.18, f32[1,1,2,384,384]{4,3,2,1,0:T(8,128)S(1)} %copy-done.10, s32[512]{0:T(512)S(1)} %pad_add_fusion, s32[384]{0:T(512)S(1)} %get-tuple-element.51), kind=kOutput, calls=%fused_computation.16 | convolution fusion | flops 453574656 | bytes 2166784 | tf_op jit(solution)/shard_map/dot_general | solution.py:293
  22.3 4.5 %all-to-all-start = ((f32[4,64,256]{2,1,0:T(8,128)}), f32[4,64,256]{2,1,0:T(8,128)S(1)}, u32[]{:S(2)}, u32[]{:S(2)}) async-start(f32[4,64,256]{2,1,0:T(8,128)} %shard_map.107), calls=%async_computation | async-start | bytes 524288 | tf_op jit(solution)/shard_map/all_to_all | solution.py:23
  26.8 3.0 %convolution_bitcast_fusion = f32[384,512]{1,0:T(8,128)} fusion(f32[384,512]{1,0:T(8,128)} %fusion.13, f32[1,1,3,384,384]{4,3,2,1,0:T(8,128)} %param.14), kind=kOutput, calls=%fused_computation.12 | convolution fusion | flops 452984832 | bytes 2162688 | tf_op jit(solution)/shard_map/dot_general | solution.py:294
  29.8 4.4 %all-to-all-done.got = f32[4,64,256]{2,1,0:T(8,128)S(1)} async-done(((f32[4,64,256]{2,1,0:T(8,128)}), f32[4,64,256]{2,1,0:T(8,128)S(1)}, u32[]{:S(2)}, u32[]{:S(2)}) %all-to-all-start) | async-done | bytes 262176 | tf_op jit(solution)/shard_map/all_to_all | solution.py:23
  34.1 1.9 %collective-permute-start.3 = (f32[64,256]{1,0:T(8,128)S(1)}, f32[64,256]{1,0:T(8,128)S(1)}, u32[]{:S(2)}, u32[]{:S(2)}) collective-permute-start(f32[64,256]{1,0:T(8,128)S(1)} %shard_map.108.mine), channel_id=1, source_target_pairs={{0,1},{1,0},{2,3},{3,2},{4,5},{5,4},{6,7},{7,6},{8,9},{9,8},{10,11... | collective-permute-start | bytes 196616 | tf_op jit(solution)/shard_map/ppermute | solution.py:315
  36.0 4.5 %fusion.schur = f32[512,512]{1,0:T(8,128)S(1)} fusion(f32[384,512]{1,0:T(8,128)} %convolution_bitcast_fusion, f32[384,512]{1,0:T(8,128)} %bitcast.54, f32[384,512]{1,0:T(8,128)} %bitcast.55), kind=kOutput, calls=%fused_computation | convolution fusion | flops 1813118976 | bytes 3407872 | tf_op jit(solution)/shard_map/dot_general | solution.py:296
  42.3 5.0 %collective-permute-start.5 = (f32[256,256]{1,0:T(8,128)S(1)}, f32[256,256]{1,0:T(8,128)S(1)}, u32[]{:S(2)}, u32[]{:S(2)}) collective-permute-start(f32[256,256]{1,0:T(8,128)S(1)} %get-tuple-element.29.right), channel_id=1, source_target_pairs={{0,8},{8,16},{16,24},{24,32},{32,40},{40,48},{48,56},{56,64},{64,7... | collective-permute-start | bytes 786440 | tf_op jit(solution)/shard_map/ppermute | solution.py:19
  47.4 5.1 %collective-permute-start.4 = (f32[256,256]{1,0:T(8,128)S(1)}, f32[256,256]{1,0:T(8,128)S(1)}, u32[]{:S(2)}, u32[]{:S(2)}) collective-permute-start(f32[256,256]{1,0:T(8,128)S(1)} %get-tuple-element.30.left), channel_id=1, source_target_pairs={{0,504},{8,0},{16,8},{24,16},{32,24},{40,32},{48,40},{56,48},{64,5... | collective-permute-start | bytes 786440 | tf_op jit(solution)/shard_map/ppermute | solution.py:19
  52.5 5.0 %collective-permute-done.5.from_prev = f32[256,256]{1,0:T(8,128)S(1)} collective-permute-done((f32[256,256]{1,0:T(8,128)S(1)}, f32[256,256]{1,0:T(8,128)S(1)}, u32[]{:S(2)}, u32[]{:S(2)}) %collective-permute-start.5) | collective-permute-done | bytes 262176 | tf_op jit(solution)/shard_map/ppermute | solution.py:19
  59.3 1.9 %collective-permute-start.6 = (f32[64,256]{1,0:T(8,128)S(1)}, f32[64,256]{1,0:T(8,128)S(1)}, u32[]{:S(2)}, u32[]{:S(2)}) collective-permute-start(f32[64,256]{1,0:T(8,128)S(1)} %get-tuple-element.34), channel_id=1, source_target_pairs={{0,1},{1,0},{2,3},{3,2},{4,5},{5,4},{6,7},{7,6},{8,9},{9,8},{10,11... | collective-permute-start | bytes 196616 | tf_op jit(solution)/shard_map/ppermute | solution.py:310
  62.5 9.7 %all_to_all.30.got = f32[4,64,256]{2,1,0:T(8,128)S(1)} all-to-all(f32[4,64,256]{2,1,0:T(8,128)S(1)} %shard_map.112), channel_id=1, replica_groups={{0,2,4,6},{1,3,5,7},{8,10,12,14},{9,11,13,15},{16,18,20,22},{17,19,21,2..., dimensions={0} | all-to-all | bytes 524288 | tf_op jit(solution)/shard_map/all_to_all | solution.py:23
  72.1 2.1 %collective-permute-start.7 = (f32[64,256]{1,0:T(8,128)S(1)}, f32[64,256]{1,0:T(8,128)S(1)}, u32[]{:S(2)}, u32[]{:S(2)}) collective-permute-start(f32[64,256]{1,0:T(8,128)S(1)} %shard_map.113.mine), channel_id=1, source_target_pairs={{0,1},{1,0},{2,3},{3,2},{4,5},{5,4},{6,7},{7,6},{8,9},{9,8},{10,11... | collective-permute-start | bytes 196616 | tf_op jit(solution)/shard_map/ppermute | solution.py:315
  76.0 3.0 %collective-permute-start.9 = (f32[256,256]{1,0:T(8,128)S(1)}, f32[256,256]{1,0:T(8,128)S(1)}, u32[]{:S(2)}, u32[]{:S(2)}) collective-permute-start(f32[256,256]{1,0:T(8,128)S(1)} %get-tuple-element.35.right), channel_id=1, source_target_pairs={{0,8},{8,16},{16,24},{24,32},{32,40},{40,48},{48,56},{56,64},{64,7... | collective-permute-start | bytes 786440 | tf_op jit(solution)/shard_map/ppermute | solution.py:19
  79.0 5.9 %collective-permute-start.8 = (f32[256,256]{1,0:T(8,128)S(1)}, f32[256,256]{1,0:T(8,128)S(1)}, u32[]{:S(2)}, u32[]{:S(2)}) collective-permute-start(f32[256,256]{1,0:T(8,128)S(1)} %get-tuple-element.36.left), channel_id=1, source_target_pairs={{0,504},{8,0},{16,8},{24,16},{32,24},{40,32},{48,40},{56,48},{64,5... | collective-permute-start | bytes 786440 | tf_op jit(solution)/shard_map/ppermute | solution.py:19
  84.9 5.0 %collective-permute-done.9.from_prev = f32[256,256]{1,0:T(8,128)S(1)} collective-permute-done((f32[256,256]{1,0:T(8,128)S(1)}, f32[256,256]{1,0:T(8,128)S(1)}, u32[]{:S(2)}, u32[]{:S(2)}) %collective-permute-start.9) | collective-permute-done | bytes 262176 | tf_op jit(solution)/shard_map/ppermute | solution.py:19
  91.1 1.5 shard_map.115
  93.4 3.4 %all-to-all-start.2 = ((f32[8,32,256]{2,1,0:T(8,128)}), f32[8,32,256]{2,1,0:T(8,128)S(1)}, u32[]{:S(2)}, u32[]{:S(2)}) async-start(f32[8,32,256]{2,1,0:T(8,128)} %get-tuple-element.37), calls=%async_computation.2 | async-start | bytes 524288 | tf_op jit(solution)/shard_map/all_to_all | solution.py:23
  97.8 1.5 shard_map.116
  100.1 4.1 %all-to-all-done.2.got = f32[8,32,256]{2,1,0:T(8,128)S(1)} async-done(((f32[8,32,256]{2,1,0:T(8,128)}), f32[8,32,256]{2,1,0:T(8,128)S(1)}, u32[]{:S(2)}, u32[]{:S(2)}) %all-to-all-start.2) | async-done | bytes 262176 | tf_op jit(solution)/shard_map/all_to_all | solution.py:23
  104.3 9.3 %all_to_all.31.gathered = f32[8,24,256]{2,1,0:T(8,128)S(1)} all-to-all(f32[8,24,256]{2,1,0:T(8,128)S(1)} %shard_map.117), channel_id=1, replica_groups=mesh['sub'=64,'grp'=8] {'grp'}, dimensions={0} | all-to-all | bytes 393216 | tf_op jit(solution)/shard_map/all_to_all | solution.py:23
  114.3 9.7 %all-to-all-start.4 = ((f32[16,8,256]{2,1,0:T(8,128)}), f32[16,8,256]{2,1,0:T(8,128)S(1)}, u32[]{:S(2)}, u32[]{:S(2)}) async-start(f32[16,8,256]{2,1,0:T(8,128)} %shard_map.118), calls=%async_computation.4 | async-start | bytes 262144 | tf_op jit(solution)/shard_map/all_to_all | solution.py:23
  124.0 1.3 shard_map.120
  125.3 2.0 %collective-permute-start.10 = (f32[256,256]{1,0:T(8,128)}, f32[256,256]{1,0:T(8,128)S(1)}, u32[]{:S(2)}, u32[]{:S(2)}) collective-permute-start(f32[256,256]{1,0:T(8,128)} %get-tuple-element.44), channel_id=1, source_target_pairs={{0,504},{8,0},{16,8},{24,16},{32,24},{40,32},{48,40},{56,48},{64,5... | collective-permute-start | bytes 786440 | tf_op jit(solution)/shard_map/ppermute | solution.py:19
  127.3 10.9 %all-to-all-done.4.got = f32[16,8,256]{2,1,0:T(8,128)S(1)} async-done(((f32[16,8,256]{2,1,0:T(8,128)}), f32[16,8,256]{2,1,0:T(8,128)S(1)}, u32[]{:S(2)}, u32[]{:S(2)}) %all-to-all-start.4) | async-done | bytes 131104 | tf_op jit(solution)/shard_map/all_to_all | solution.py:23
  138.8 5.0 %all-to-all-start.5 = ((f32[4,8,256]{2,1,0:T(8,128)}), f32[4,8,256]{2,1,0:T(8,128)S(1)}, u32[]{:S(2)}, u32[]{:S(2)}) async-start(f32[4,8,256]{2,1,0:T(8,128)} %shard_map.119), calls=%async_computation.5 | async-start | bytes 65536 | tf_op jit(solution)/shard_map/all_to_all | solution.py:23
  143.9 5.4 %all-to-all-done.5.sums = f32[4,8,256]{2,1,0:T(8,128)S(1)} async-done(((f32[4,8,256]{2,1,0:T(8,128)}), f32[4,8,256]{2,1,0:T(8,128)S(1)}, u32[]{:S(2)}, u32[]{:S(2)}) %all-to-all-start.5) | async-done | bytes 32800 | tf_op jit(solution)/shard_map/all_to_all | solution.py:23
  (55 shorter events, 17.1 us)
Async XLA Ops:
  0.6 13.9 %copy-start = (f32[1,1,3,384,128]{4,3,2,1,0:T(8,128)S(1)}, f32[1,1,3,384,128]{4,3,2,1,0:T(8,128)}, u32[]{:S(2)}) copy-start(f32[1,1,3,384,128]{4,3,2,1,0:T(8,128)} %param.16) | copy-start | bytes 1769476
  0.6 10.9 %copy-start.10 = (f32[1,1,2,384,384]{4,3,2,1,0:T(8,128)S(1)}, f32[1,1,2,384,384]{4,3,2,1,0:T(8,128)}, u32[]{:S(2)}) copy-start(f32[1,1,2,384,384]{4,3,2,1,0:T(8,128)} %param.15) | copy-start | bytes 3538948
  1.5 15.8 %collective-permute-start.1 = (f32[8,256]{1,0:T(8,128)S(1)}, f32[8,256]{1,0:T(8,128)S(1)}, u32[]{:S(2)}, u32[]{:S(2)}) collective-permute-start(f32[8,256]{1,0:T(8,128)S(1)} %broadcast_in_dim.6), channel_id=1, source_target_pairs={{0,8},{8,16},{16,24},{24,32},{32,40},{40,48},{48,56},{56,64},{64,7... | collective-permute-start | bytes 24584 | tf_op jit(solution)/shard_map/ppermute | solution.py:19
  5.3 12.0 %collective-permute-start = (f32[256,256]{1,0:T(8,128)}, f32[256,256]{1,0:T(8,128)S(1)}, u32[]{:S(2)}, u32[]{:S(2)}) collective-permute-start(f32[256,256]{1,0:T(8,128)} %bitcast.48), channel_id=1, source_target_pairs={{0,8},{8,16},{16,24},{24,32},{32,40},{40,48},{48,56},{56,64},{64,7... | collective-permute-start | bytes 786440 | tf_op jit(solution)/shard_map/ppermute | solution.py:19
  11.6 2.7 %copy-start.9 = (f32[512,384]{0,1:T(8,128)}, f32[512,384]{0,1:T(8,128)S(1)}, u32[]{:S(2)}) copy-start(f32[512,384]{0,1:T(8,128)S(1)} %fusion.15) | copy-start | bytes 2359300
  14.3 7.3 %copy-start.8 = (f32[512,384]{0,1:T(8,128)}, f32[512,384]{0,1:T(8,128)S(1)}, u32[]{:S(2)}) copy-start(f32[512,384]{0,1:T(8,128)S(1)} %fusion.18) | copy-start | bytes 2359300
  14.6 2.2 %copy-start.11 = (f32[1,128,128]{2,1,0:T(8,128)S(1)}, f32[1,128,128]{2,1,0:T(8,128)}, u32[]{:S(2)}) copy-start(f32[1,128,128]{2,1,0:T(8,128)} %param.17) | copy-start | bytes 196612
  14.6 2.6 %copy-start.6 = (f32[1,1,256]{2,1,0:T(1,128)S(1)}, f32[1,1,256]{2,1,0:T(1,128)}, u32[]{:S(2)}) copy-start(f32[1,1,256]{2,1,0:T(1,128)} %param.11) | copy-start | bytes 3076
  14.6 2.6 %copy-start.7 = (s32[1,1,256]{2,1,0:T(1,128)S(1)}, s32[1,1,256]{2,1,0:T(1,128)}, u32[]{:S(2)}) copy-start(s32[1,1,256]{2,1,0:T(1,128)} %param.10) | copy-start | bytes 3076
  14.6 2.7 %copy-start.1 = (f32[1,1,256,256]{3,2,1,0:T(8,128)S(1)}, f32[1,1,256,256]{3,2,1,0:T(8,128)}, u32[]{:S(2)}) copy-start(f32[1,1,256,256]{3,2,1,0:T(8,128)} %param.9) | copy-start | bytes 786436
  17.9 3.6 %collective-permute-start.2 = (f32[64,256]{1,0:T(8,128)S(1)}, f32[64,256]{1,0:T(8,128)S(1)}, u32[]{:S(2)}, u32[]{:S(2)}) collective-permute-start(f32[64,256]{1,0:T(8,128)S(1)} %get-tuple-element.28), channel_id=1, source_target_pairs={{0,1},{1,0},{2,3},{3,2},{4,5},{5,4},{6,7},{7,6},{8,9},{9,8},{10,11... | collective-permute-start | bytes 196616 | tf_op jit(solution)/shard_map/ppermute | solution.py:310
  22.3 11.8 %all-to-all-start = ((f32[4,64,256]{2,1,0:T(8,128)}), f32[4,64,256]{2,1,0:T(8,128)S(1)}, u32[]{:S(2)}, u32[]{:S(2)}) async-start(f32[4,64,256]{2,1,0:T(8,128)} %shard_map.107), calls=%async_computation | async-start | bytes 524288 | tf_op jit(solution)/shard_map/all_to_all | solution.py:23
  34.1 7.6 %collective-permute-start.3 = (f32[64,256]{1,0:T(8,128)S(1)}, f32[64,256]{1,0:T(8,128)S(1)}, u32[]{:S(2)}, u32[]{:S(2)}) collective-permute-start(f32[64,256]{1,0:T(8,128)S(1)} %shard_map.108.mine), channel_id=1, source_target_pairs={{0,1},{1,0},{2,3},{3,2},{4,5},{5,4},{6,7},{7,6},{8,9},{9,8},{10,11... | collective-permute-start | bytes 196616 | tf_op jit(solution)/shard_map/ppermute | solution.py:315
  42.3 15.2 %collective-permute-start.5 = (f32[256,256]{1,0:T(8,128)S(1)}, f32[256,256]{1,0:T(8,128)S(1)}, u32[]{:S(2)}, u32[]{:S(2)}) collective-permute-start(f32[256,256]{1,0:T(8,128)S(1)} %get-tuple-element.29.right), channel_id=1, source_target_pairs={{0,8},{8,16},{16,24},{24,32},{32,40},{40,48},{48,56},{56,64},{64,7... | collective-permute-start | bytes 786440 | tf_op jit(solution)/shard_map/ppermute | solution.py:19
  47.4 11.3 %collective-permute-start.4 = (f32[256,256]{1,0:T(8,128)S(1)}, f32[256,256]{1,0:T(8,128)S(1)}, u32[]{:S(2)}, u32[]{:S(2)}) collective-permute-start(f32[256,256]{1,0:T(8,128)S(1)} %get-tuple-element.30.left), channel_id=1, source_target_pairs={{0,504},{8,0},{16,8},{24,16},{32,24},{40,32},{48,40},{56,48},{64,5... | collective-permute-start | bytes 786440 | tf_op jit(solution)/shard_map/ppermute | solution.py:19
  59.3 3.1 %collective-permute-start.6 = (f32[64,256]{1,0:T(8,128)S(1)}, f32[64,256]{1,0:T(8,128)S(1)}, u32[]{:S(2)}, u32[]{:S(2)}) collective-permute-start(f32[64,256]{1,0:T(8,128)S(1)} %get-tuple-element.34), channel_id=1, source_target_pairs={{0,1},{1,0},{2,3},{3,2},{4,5},{5,4},{6,7},{7,6},{8,9},{9,8},{10,11... | collective-permute-start | bytes 196616 | tf_op jit(solution)/shard_map/ppermute | solution.py:310
  72.1 3.2 %collective-permute-start.7 = (f32[64,256]{1,0:T(8,128)S(1)}, f32[64,256]{1,0:T(8,128)S(1)}, u32[]{:S(2)}, u32[]{:S(2)}) collective-permute-start(f32[64,256]{1,0:T(8,128)S(1)} %shard_map.113.mine), channel_id=1, source_target_pairs={{0,1},{1,0},{2,3},{3,2},{4,5},{5,4},{6,7},{7,6},{8,9},{9,8},{10,11... | collective-permute-start | bytes 196616 | tf_op jit(solution)/shard_map/ppermute | solution.py:315
  76.0 13.9 %collective-permute-start.9 = (f32[256,256]{1,0:T(8,128)S(1)}, f32[256,256]{1,0:T(8,128)S(1)}, u32[]{:S(2)}, u32[]{:S(2)}) collective-permute-start(f32[256,256]{1,0:T(8,128)S(1)} %get-tuple-element.35.right), channel_id=1, source_target_pairs={{0,8},{8,16},{16,24},{24,32},{32,40},{40,48},{48,56},{56,64},{64,7... | collective-permute-start | bytes 786440 | tf_op jit(solution)/shard_map/ppermute | solution.py:19
  79.0 12.1 %collective-permute-start.8 = (f32[256,256]{1,0:T(8,128)S(1)}, f32[256,256]{1,0:T(8,128)S(1)}, u32[]{:S(2)}, u32[]{:S(2)}) collective-permute-start(f32[256,256]{1,0:T(8,128)S(1)} %get-tuple-element.36.left), channel_id=1, source_target_pairs={{0,504},{8,0},{16,8},{24,16},{32,24},{40,32},{48,40},{56,48},{64,5... | collective-permute-start | bytes 786440 | tf_op jit(solution)/shard_map/ppermute | solution.py:19
  92.6 0.8 copy-start.2
  93.4 10.9 %all-to-all-start.2 = ((f32[8,32,256]{2,1,0:T(8,128)}), f32[8,32,256]{2,1,0:T(8,128)S(1)}, u32[]{:S(2)}, u32[]{:S(2)}) async-start(f32[8,32,256]{2,1,0:T(8,128)} %get-tuple-element.37), calls=%async_computation.2 | async-start | bytes 524288 | tf_op jit(solution)/shard_map/all_to_all | solution.py:23
  96.8 1.0 copy-start.3
  99.3 0.8 copy-start.4
  104.2 19.8 %copy-start.5 = (f32[512,256]{1,0:T(8,128)S(1)}, f32[512,256]{1,0:T(8,128)}, u32[]{:S(2)}) copy-start(f32[512,256]{1,0:T(8,128)} %copy-done.4) | copy-start | bytes 1572868
  114.3 23.9 %all-to-all-start.4 = ((f32[16,8,256]{2,1,0:T(8,128)}), f32[16,8,256]{2,1,0:T(8,128)S(1)}, u32[]{:S(2)}, u32[]{:S(2)}) async-start(f32[16,8,256]{2,1,0:T(8,128)} %shard_map.118), calls=%async_computation.4 | async-start | bytes 262144 | tf_op jit(solution)/shard_map/all_to_all | solution.py:23
  125.3 18.6 %collective-permute-start.10 = (f32[256,256]{1,0:T(8,128)}, f32[256,256]{1,0:T(8,128)S(1)}, u32[]{:S(2)}, u32[]{:S(2)}) collective-permute-start(f32[256,256]{1,0:T(8,128)} %get-tuple-element.44), channel_id=1, source_target_pairs={{0,504},{8,0},{16,8},{24,16},{32,24},{40,32},{48,40},{56,48},{64,5... | collective-permute-start | bytes 786440 | tf_op jit(solution)/shard_map/ppermute | solution.py:19
  138.8 10.5 %all-to-all-start.5 = ((f32[4,8,256]{2,1,0:T(8,128)}), f32[4,8,256]{2,1,0:T(8,128)S(1)}, u32[]{:S(2)}, u32[]{:S(2)}) async-start(f32[4,8,256]{2,1,0:T(8,128)} %shard_map.119), calls=%async_computation.5 | async-start | bytes 65536 | tf_op jit(solution)/shard_map/all_to_all | solution.py:23
